TPU v7x, 256 devices: a whole 4x4x8 slice. The times are simulated.
256 devices in a mesh: panel: 32 (over z, y_lo, core), rep: 8 (over x, y_hi).
Axes of the slice: x: 4, y: 4 (y_hi: 2, y_lo: 2; y = y_hi * 2 + y_lo), z: 8, core: 2. Of those that a mesh axis runs over, the one named last changes fastest.
Arguments:
- x_src: bfloat16 [4096, 128], P('panel'), may hold values from -6 to 6
- x_dst: bfloat16 [131072, 128], P(('panel', 'rep')), may hold values from -6 to 6
- weight: bfloat16 [128, 512], replicated, may hold values from -0.5 to 0.5
- att_src: float32 [8, 64], replicated, may hold values from -0.75 to 0.75
- att_dst: float32 [8, 64], replicated, may hold values from -0.75 to 0.75
- grad_out: bfloat16 [131072, 512], P(('panel', 'rep')), may hold values from -6 to 6
- block_rows: int32 [4096], P(('panel', 'rep')), may hold values from 0 to 3, as said below
- block_cols: int32 [4096], P(('panel', 'rep')), may hold values from 0 to 31
- block_masks: int32 [4096, 128, 128], P(('panel', 'rep')), may hold values from 0 to 1, as said below
- block_counts: int32 [256], P(('panel', 'rep')), may hold values from 2 to 16, as said below
Outputs:
- grad_src: float32 [4096, 128], P('panel')
- grad_dst: float32 [131072, 128], P(('panel', 'rep'))
- grad_weight: float32 [128, 512], replicated
- grad_att_src: float32 [8, 64], replicated
- grad_att_dst: float32 [8, 64], replicated
Inputs may be any that keep to these rules, and one draw needn't show every extreme that they name: `block_counts`: live block slots of one device; at least one device has exactly 16. The pairs of block_rows and block_cols within one device's 16 slots are distinct. `block_masks`: slots at or after a device's count of live blocks hold only zeros.
All inputs are finite; a program needn't handle non-finite values.
Results may differ from a plain program's by a relative error of at most 0.012.
The roundings to bfloat16 on the way count: a program that leaves them out, or rounds other values in their place, can miss the bound.
Values may be sent and summed in bfloat16 or wider, within the bound.
No kernel may reach another device: no remote copies, remote signals or barrier semaphores. Data moves between devices by JAX's collectives and lax.ppermute only.
A program may use at most 128 MiB of HBM per device.

v0:
```python
import math

import jax
import jax.numpy as jnp
from jax import lax
from jax.sharding import PartitionSpec as P

HIGHEST_PRECISION = lax.Precision.HIGHEST


def smooth_leaky(values):
    return 0.2 * values + 0.8 * jax.nn.softplus(values)


def smooth_slope(values):
    return 0.2 + 0.8 * jax.nn.sigmoid(values)


def shards(
    x_src,
    x_dst,
    weight,
    att_src,
    att_dst,
    grad_out,
    block_rows,
    block_cols,
    block_masks,
    block_counts,
):
    num_heads, head_dim = att_src.shape
    model_width = weight.shape[1]
    block_size = block_masks.shape[1]
    dest_count = x_dst.shape[0]
    source_local = x_src.shape[0]
    slot_count = block_rows.shape[0]
    proj_own = jnp.dot(x_src, weight, preferred_element_type=jnp.float32).astype(jnp.bfloat16)
    proj_all = lax.all_gather(proj_own, "panel", axis=0, tiled=True)
    source_total = proj_all.shape[0]
    dest_blocks = dest_count // block_size
    source_blocks = source_total // block_size
    source_feats = proj_all.reshape(source_total, num_heads, head_dim)
    score_src = jnp.einsum(
        "jhk,hk->hj", source_feats.astype(jnp.float32), att_src, precision=HIGHEST_PRECISION
    )
    proj_dst = jnp.dot(x_dst, weight, preferred_element_type=jnp.float32).astype(jnp.bfloat16)
    feats = proj_dst.reshape(dest_count, num_heads, head_dim)
    feats_wide = feats.astype(jnp.float32)
    score_d = jnp.einsum("ihk,hk->hi", feats_wide, att_dst, precision=HIGHEST_PRECISION)
    score_own = jnp.einsum("ihk,hk->hi", feats_wide, att_src, precision=HIGHEST_PRECISION)
    cotan = grad_out.reshape(dest_count, num_heads, head_dim)
    cotan_wide = cotan.astype(jnp.float32)
    live_count = block_counts[0]
    score_d_blocks = score_d.reshape(num_heads, dest_blocks, block_size)
    score_src_blocks = score_src.reshape(num_heads, source_blocks, block_size)
    source_row_blocks = source_feats.reshape(source_blocks, block_size, num_heads, head_dim)
    cotan_blocks = cotan.reshape(dest_blocks, block_size, num_heads, head_dim)
    group = math.gcd(slot_count, 16)
    groups = slot_count // group
    alive_all = (jnp.arange(slot_count, dtype=jnp.int32) < live_count).astype(jnp.float32)
    slot_inputs = (
        block_rows.reshape(groups, group),
        block_cols.reshape(groups, group),
        block_masks.reshape(groups, group, block_size, block_size),
        alive_all.reshape(groups, group),
    )

    def group_scores(rows, cols, masks, alive):
        dest_hot = (rows[:, None] == jnp.arange(dest_blocks, dtype=jnp.int32)[None, :]).astype(
            jnp.float32
        )
        source_hot = (cols[:, None] == jnp.arange(source_blocks, dtype=jnp.int32)[None, :]).astype(
            jnp.float32
        )
        score_rows = jnp.einsum(
            "gd,hdu->ghu", dest_hot, score_d_blocks, precision=HIGHEST_PRECISION
        )
        score_cols = jnp.einsum(
            "gs,hsv->ghv", source_hot, score_src_blocks, precision=HIGHEST_PRECISION
        )
        pre_score = score_rows[:, :, :, None] + score_cols[:, :, None, :]
        edge_mask = masks.astype(jnp.float32) * alive[:, None, None]
        edge_weight = jnp.exp(smooth_leaky(pre_score)) * edge_mask[:, None]
        source_rows = jnp.take(source_row_blocks, cols, axis=0)
        return (dest_hot, source_hot, pre_score, edge_weight, source_rows)

    def forward_group(carried_fwd, slot_group):
        denominator, numerator = carried_fwd
        rows, cols, masks, alive = slot_group
        dest_hot, source_hot, pre_score, edge_weight, source_rows = group_scores(
            rows, cols, masks, alive
        )
        part_num = jnp.einsum(
            "ghij,gjhk->gihk",
            edge_weight.astype(jnp.bfloat16),
            source_rows,
            preferred_element_type=jnp.float32,
        )
        denominator = denominator + jnp.einsum(
            "gd,ghi->hdi", dest_hot, edge_weight.sum(axis=3), precision=HIGHEST_PRECISION
        )
        numerator = numerator + jnp.einsum(
            "gd,gihk->dihk", dest_hot, part_num, precision=HIGHEST_PRECISION
        )
        return ((denominator, numerator), None)

    (denominator_blocks, numerator_blocks), _ = lax.scan(
        forward_group,
        (
            jnp.zeros((num_heads, dest_blocks, block_size), jnp.float32),
            jnp.zeros((dest_blocks, block_size, num_heads, head_dim), jnp.float32),
        ),
        slot_inputs,
    )
    denominator = denominator_blocks.reshape(num_heads, dest_count)
    numerator = numerator_blocks.reshape(dest_count, num_heads, head_dim)
    pre_self = score_d + score_own
    self_weight = jnp.exp(smooth_leaky(pre_self))
    denominator = denominator + self_weight
    numerator = numerator + self_weight.T[:, :, None] * feats_wide
    attended = numerator / denominator.T[:, :, None]
    centred = jnp.sum(cotan_wide * attended, axis=2).T
    denominator_full = denominator.reshape(num_heads, dest_blocks, block_size)
    centred_full = centred.reshape(num_heads, dest_blocks, block_size)

    def backward_group(carried_bwd, slot_group):
        grad_source, grad_score_src, grad_score_dst = carried_bwd
        rows, cols, masks, alive = slot_group
        dest_hot, source_hot, pre_score, edge_weight, source_rows = group_scores(
            rows, cols, masks, alive
        )
        denom_rows = jnp.einsum(
            "gd,hdi->ghi", dest_hot, denominator_full, precision=HIGHEST_PRECISION
        )
        attention = edge_weight / denom_rows[:, :, :, None]
        cotan_rows = jnp.take(cotan_blocks, rows, axis=0)
        pair_grad = jnp.einsum(
            "gihk,gjhk->ghij", cotan_rows, source_rows, preferred_element_type=jnp.float32
        )
        centred_rows = jnp.einsum(
            "gd,hdi->ghi", dest_hot, centred_full, precision=HIGHEST_PRECISION
        )
        score_grad = attention * (pair_grad - centred_rows[:, :, :, None]) * smooth_slope(pre_score)
        feat_grad = jnp.einsum(
            "ghij,gihk->gjhk",
            attention.astype(jnp.bfloat16),
            cotan_rows,
            preferred_element_type=jnp.float32,
        )
        grad_source = grad_source + jnp.einsum(
            "gs,gjhk->sjhk", source_hot, feat_grad, precision=HIGHEST_PRECISION
        )
        grad_score_src = grad_score_src + jnp.einsum(
            "gs,ghj->hsj", source_hot, score_grad.sum(axis=2), precision=HIGHEST_PRECISION
        )
        grad_score_dst = grad_score_dst + jnp.einsum(
            "gd,ghi->hdi", dest_hot, score_grad.sum(axis=3), precision=HIGHEST_PRECISION
        )
        return ((grad_source, grad_score_src, grad_score_dst), None)

    (grad_source_blocks, grad_score_src_blocks, grad_score_dst_blocks), _ = lax.scan(
        backward_group,
        (
            jnp.zeros((source_blocks, block_size, num_heads, head_dim), jnp.float32),
            jnp.zeros((num_heads, source_blocks, block_size), jnp.float32),
            jnp.zeros((num_heads, dest_blocks, block_size), jnp.float32),
        ),
        slot_inputs,
    )
    grad_source = grad_source_blocks.reshape(source_total, num_heads, head_dim)
    grad_score_src = grad_score_src_blocks.reshape(num_heads, source_total)
    grad_score_dst = grad_score_dst_blocks.reshape(num_heads, dest_count)
    self_attention = self_weight / denominator
    self_pair = jnp.sum(cotan_wide * feats_wide, axis=2).T
    self_grad = self_attention * (self_pair - centred) * smooth_slope(pre_self)
    grad_score_dst = grad_score_dst + self_grad
    grad_dest = (
        self_attention.T[:, :, None] * cotan_wide
        + self_grad.T[:, :, None] * att_src[None]
        + grad_score_dst.T[:, :, None] * att_dst[None]
    )
    grad_source = grad_source + grad_score_src.T[:, :, None] * att_src[None]
    att_src_part = jnp.einsum(
        "hj,jhk->hk", grad_score_src, source_feats.astype(jnp.float32), precision=HIGHEST_PRECISION
    ) + jnp.einsum("hi,ihk->hk", self_grad, feats_wide, precision=HIGHEST_PRECISION)
    att_dst_part = jnp.einsum("hi,ihk->hk", grad_score_dst, feats_wide, precision=HIGHEST_PRECISION)
    weight_t = weight.astype(jnp.float32).T
    source_flat = grad_source.reshape(source_total, model_width)
    dest_flat = grad_dest.reshape(dest_count, model_width)
    grad_dst = jnp.dot(dest_flat, weight_t, precision=HIGHEST_PRECISION)
    weight_part = jnp.dot(x_dst.astype(jnp.float32).T, dest_flat, precision=HIGHEST_PRECISION)
    share_rows = source_local // lax.axis_size("rep")
    share_start = lax.axis_index("rep") * share_rows
    panel_part = lax.psum_scatter(source_flat, "panel", scatter_dimension=0, tiled=True)
    panel_sum = lax.psum(panel_part, "rep")
    own_share = lax.dynamic_slice_in_dim(panel_sum, share_start, share_rows, 0)
    grad_src = jnp.dot(panel_sum, weight_t, precision=HIGHEST_PRECISION)
    own_inputs = lax.dynamic_slice_in_dim(x_src, share_start, share_rows, 0).astype(jnp.float32)
    weight_part = weight_part + jnp.dot(own_inputs.T, own_share, precision=HIGHEST_PRECISION)
    grad_weight, grad_att_src, grad_att_dst = lax.psum(
        (weight_part, att_src_part, att_dst_part), ("panel", "rep")
    )
    return (grad_src, grad_dst, grad_weight, grad_att_src, grad_att_dst)


def solution(mesh):
    return jax.shard_map(
        shards,
        mesh=mesh,
        in_specs=(
            P("panel", None),
            P(("panel", "rep"), None),
            P(),
            P(),
            P(),
            P(("panel", "rep"), None),
            P(("panel", "rep")),
            P(("panel", "rep")),
            P(("panel", "rep"), None, None),
            P(("panel", "rep")),
        ),
        out_specs=(P("panel", None), P(("panel", "rep"), None), P(), P(), P()),
        check_vma=False,
    )
```

profile of v0, /device:TPU:1, one launch (start us, length us, event | category | flops | bytes accessed | tf_op | source)
XLA Modules:
  0.0 674.2 jit_solution(18316904664663348412)
XLA Ops:
  9.7 2.1 copy.48
  20.7 2.4 convert_multiply_fusion.2
  23.1 58.5 %all-gather.2.cloned.1.call-done = bf16[4096,512]{1,0:T(8,128)(2,1)} async-done(((bf16[128,512]{1,0:T(8,128)(2,1)}), bf16[4096,512]{1,0:T(8,128)(2,1)}) %all-gather.2.cloned.1.call-update) | async-done | bytes 4194320 | tf_op jit(solution)/shard_map/all_gather | solution.py:38
  81.5 6.4 copy.41
  87.9 3.9 fusion.99
  92.2 9.5 %fusion.23 = f32[16,8,128]{2,1,0:T(8,128)S(1)} fusion(f32[16,128,128]{2,1,0:T(8,128)} %convert_multiply_fusion.2, f32[16,8,128]{2,1,0:T(8,128)S(1)} %copy.42, f32[16,8,128]{2,1,0:T(8,128)S(1)} %copy.40), kind=kLoop, calls=%fused_computation.33 | loop fusion | flops 25149440 | bytes 1245184 | tf_op jit(solution)/shard_map/while/body/eval_jaxpr/reduce_sum | solution.py:100
  101.9 11.2 %reshape.149 = bf16[32,128,8,64]{3,2,1,0:T(8,128)(2,1)} reshape(bf16[4096,512]{1,0:T(8,128)(2,1)} %all-gather.2.cloned.1.call-done) | data formatting | bytes 8388608 | tf_op jit(solution)/shard_map/reshape;reshape | solution.py:56
  113.1 9.1 %copy.47 = bf16[32,128,8,64]{1,3,2,0:T(8,128)(2,1)} copy(bf16[32,128,8,64]{3,2,1,0:T(8,128)(2,1)} %reshape.149) | data formatting | bytes 8388608 | tf_op jit(solution)/shard_map/reshape;reshape | solution.py:56
  122.2 4.3 gather_fusion.1
  126.5 9.6 %fusion.27 = f32[16,128,8,64]{1,3,2,0:T(8,128)S(1)} fusion(f32[16,128,128]{2,1,0:T(8,128)} %convert_multiply_fusion.2, f32[16,8,128]{2,1,0:T(8,128)S(1)} %copy.42, f32[16,8,128]{2,1,0:T(8,128)S(1)} %copy.40, bf16[16,128,8,64]{1,3,2,0:T(8,128)(2,1)} %gather_fusion.1, pred[16]{0:T(512)(128)(4,1)S(1)} %get-tuple-element.104), kind=kOutput, calls=%fused_computation.35 | convolution fusion | flops 294649856 | bytes 7471120 | tf_op jit(solution)/shard_map/while/body/eval_jaxpr/ghij,gjhk->gihk/dot_general | solution.py:93
  136.1 5.0 fusion.14
  141.1 2.6 reshape.108
  145.9 11.8 %fusion.24 = f32[16,128,8,64]{1,3,2,0:T(8,128)S(1)} fusion(f32[16,8,128]{2,1,0:T(8,128)S(1)} %copy.44, f32[16,128,128]{2,1,0:T(8,128)} %convert_multiply_fusion.2, f32[16,8,128]{2,1,0:T(8,128)S(1)} %copy.42, f32[16,8,128]{2,1,0:T(8,128)S(1)} %copy.40, bf16[16,128,8,64]{1,3,2,0:T(8,128)(2,1)S(1)} %gather_fusion, pred[16]{0:T(512)(128)(4,1)S(1)} %get-tuple-element.105), kind=kOutput, calls=%fused_computation.34 | convolution fusion | flops 296747008 | bytes 7536656 | tf_op jit(solution)/shard_map/while/body/eval_jaxpr/ghij,gihk->gjhk/dot_general | solution.py:144
  157.7 15.5 %fusion.96 = (f32[16,8,128]{2,1,0:T(8,128)S(1)}, f32[16,8,128]{2,1,0:T(8,128)S(1)}) fusion(f32[16,8,128]{2,1,0:T(8,128)S(1)} %copy.50, bf16[16,128,8,64]{1,3,2,0:T(8,128)(2,1)S(1)} %copy-done.1, pred[16]{0:T(512)(128)(4,1)S(1)} %get-tuple-element.104, bf16[16,128,8,64]{1,3,2,0:T(8,128)(2,1)S(1)} %gather_fusion, pred[16]{0:T(512)(128)(4,1)S(1)} %get-tuple-element.105, ...), kind=kOutput, calls=%fused_computation.128 | convolution fusion | flops 316637184 | bytes 5636128 | tf_op jit(solution)/shard_map/while/body/eval_jaxpr/gihk,gjhk->ghij/dot_general | solution.py:137
  173.6 5.8 fusion.16
  179.4 12.1 %bitcast_add_fusion = f32[4096,512]{0,1:T(8,128)} fusion(f32[64,8,32,128]{3,2,1,0:T(8,128)S(1)} %bitcast.176, f32[512]{0:T(512)S(1)} %mul.185, f32[4096,8]{0,1:T(8,128)S(1)} %bitcast.183), kind=kLoop, calls=%fused_computation.22 | loop fusion | flops 4194304 | bytes 16910336 | tf_op jit(solution)/shard_map/add | solution.py:182
  193.9 5.1 fusion.103
  199.0 118.8 %reduce-scatter.2.cloned.1.call-done = f32[128,512]{0,1:T(8,128)} async-done(((f32[4096,512]{0,1:T(8,128)}), f32[128,512]{0,1:T(8,128)}) %reduce-scatter.2.cloned.1.call-update) | async-done | bytes 262160 | tf_op jit(solution)/shard_map/reduce_scatter | solution.py:194
  318.4 80.4 %all-reduce = (f32[8,64]{1,0:T(8,128)}, f32[8,64]{1,0:T(8,128)}) all-reduce(f32[8,64]{1,0:T(8,128)S(1)} %add.168, f32[8,64]{1,0:T(8,128)S(1)} %bitcast.197), channel_id=1, replica_groups=mesh['panel'=32,'rep'=8] {'panel','rep'}, use_global_device_ids=true, to_apply=%region_8.10 | all-reduce | flops 1024 | bytes 8192 | tf_op jit(solution)/shard_map/psum | solution.py:200
  400.5 6.3 all-reduce.4.cloned.1.call-done
  406.7 2.0 convolution_add_fusion
  408.7 2.0 fusion.101
  410.7 254.7 %all-reduce.6.cloned.1.call-done = f32[128,512]{0,1:T(8,128)} async-done(((f32[128,512]{0,1:T(8,128)}), f32[128,512]{0,1:T(8,128)}) %all-reduce.6.cloned.1.call-update) | async-done | bytes 262160 | tf_op jit(solution)/shard_map/psum | solution.py:200
  665.4 1.8 copy.54
  (71 shorter events, 18.4 us)
Async XLA Ops:
  7.2 0.9 copy-start
  7.2 13.2 %copy-start.7 = (s32[16]{0:T(128)S(1)}, s32[16]{0:T(128)}, u32[]{:S(2)}) copy-start(s32[16]{0:T(128)} %param.18) | copy-start | bytes 196
  7.2 13.2 %copy-start.6 = (f32[8,64]{1,0:T(8,128)S(1)}, f32[8,64]{1,0:T(8,128)}, u32[]{:S(2)}) copy-start(f32[8,64]{1,0:T(8,128)} %param.15) | copy-start | bytes 6148
  7.2 13.1 %copy-start.9 = (s32[16]{0:T(128)S(1)}, s32[16]{0:T(128)}, u32[]{:S(2)}) copy-start(s32[16]{0:T(128)} %param.19) | copy-start | bytes 196
  7.2 74.3 %all-gather.2.cloned.1.call-start = ((), (), s32[]{:S(2)}) async-start(), calls=%async_computation.1 | async-start | bytes 4325376 | tf_op jit(solution)/shard_map/all_gather | solution.py:38
  9.7 308.1 %reduce-scatter.2.cloned.1.call-start = ((), (), s32[]{:S(2)}) async-start(), calls=%async_computation.2 | async-start | bytes 8650752 | tf_op jit(solution)/shard_map/reduce_scatter | solution.py:194
  126.5 17.2 %copy-start.2 = (bf16[512,512]{0,1:T(8,128)(2,1)S(1)}, bf16[512,512]{0,1:T(8,128)(2,1)}, u32[]{:S(2)}) copy-start(bf16[512,512]{0,1:T(8,128)(2,1)} %copy.48) | copy-start | bytes 1572868
  145.9 11.8 %copy-start.1 = (bf16[16,128,8,64]{1,3,2,0:T(8,128)(2,1)S(1)}, bf16[16,128,8,64]{1,3,2,0:T(8,128)(2,1)}, u32[]{:S(2)}) copy-start(bf16[16,128,8,64]{1,3,2,0:T(8,128)(2,1)} %gather_fusion.1) | copy-start | bytes 6291460
  145.9 11.8 %copy-start.4 = (f32[16,128,128]{2,1,0:T(8,128)S(1)}, f32[16,128,128]{2,1,0:T(8,128)}, u32[]{:S(2)}) copy-start(f32[16,128,128]{2,1,0:T(8,128)} %convert_multiply_fusion.2) | copy-start | bytes 3145732
  191.5 0.7 copy-start.8
  191.5 1.1 copy-start.3
  191.5 1.8 copy-start.5
  191.5 215.2 %all-reduce.4.cloned.1.call-start = ((), (), s32[]{:S(2)}) async-start(), calls=%async_computation.3 | async-start | bytes 524288 | tf_op jit(solution)/shard_map/psum | solution.py:195
  317.8 347.6 %all-reduce.6.cloned.1.call-start = ((), (), s32[]{:S(2)}) async-start(), calls=%async_computation.4 | async-start | bytes 524288 | tf_op jit(solution)/shard_map/psum | solution.py:200
Sparse Core Ops, SparseCore 0:
  10.5 71.0 all-gather.1
  191.6 126.1 reduce-scatter.1
  320.4 86.2 all-reduce.3
  413.5 251.9 all-reduce.5
where the time goes:
time: 682 us; the launch traced here: 674 us
  waiting for transfers between devices  438 us (64%)
  blocking collectives  80.4 us (12%)
  matrix products  70.2 us (10%)
  local copies, waits for them, and re-layouts  43.3 us (6%)
  other arithmetic  26.5 us (4%)
  between operations  15.2 us (2%)
    psum x1, waiting for transfers between devices, shards(): lax.psum((weight_part, att_src_part, att_dst_part), ('panel', 'rep'))  255 us
    reduce_scatter x1, waiting for transfers between devices, shards(): lax.psum_scatter(source_flat, 'panel', scatter_dimension=0, tiled=True)  119 us
    psum x1, blocking collectives, shards(): lax.psum((weight_part, att_src_part, att_dst_part), ('panel', 'rep'))  80.4 us
    all_gather x1, waiting for transfers between devices, shards(): proj_all = lax.all_gather(proj_own, 'panel', axis=0, tiled=True)  58.5 us
    another operation x2, local copies, waits for them, and re-layouts, shards(): source_feats.reshape(source_blocks, block_size, num_heads, head_dim)  20.2 us
    dot_general x1, matrix products, backward_group(): jnp.einsum('gihk,gjhk->ghij', cotan_rows, source_rows, preferred_element_...  15.5 us
  transfers between devices with their start and end apart: 4, of which 4 were waited for; matrix products, arithmetic and copies ran while one was open for 3% of the time, Pallas kernels for 0%

commit v1 on v0

v1 whole, which is shorter than its diff:
```python
import jax
import jax.numpy as jnp
from jax import lax
from jax.experimental import pallas as pl
from jax.experimental.pallas import tpu as pltpu
from jax.sharding import PartitionSpec as P

HEADS, HEAD_DIM, IN, WIDTH, BLK = 8, 64, 128, 512, 128
LOG2E = 1.4426950408889634
LANES = 128
F32, BF16 = jnp.float32, jnp.bfloat16
VMEM_BYTES = 40 << 20
SPREAD = 32

NN = (((1,), (0,)), ((), ()))
NT = (((1,), (1,)), ((), ()))
TN = (((0,), (0,)), ((), ()))


def mm(a, b, dims=NN):
    return lax.dot_general(a, b, dims, preferred_element_type=F32)


def split2(values):
    hi = values.astype(BF16)
    return hi, (values - hi.astype(F32)).astype(BF16)


def split3(values):
    hi = values.astype(BF16)
    rest = values - hi.astype(F32)
    mid = rest.astype(BF16)
    return hi, mid, (rest - mid.astype(F32)).astype(BF16)


def head_rows(att_flat):
    head = lax.broadcasted_iota(jnp.int32, (HEADS, WIDTH), 0)
    lane = lax.broadcasted_iota(jnp.int32, (HEADS, WIDTH), 1) // HEAD_DIM
    return jnp.where(head == lane, jnp.broadcast_to(att_flat, (HEADS, WIDTH)), 0.0)


def per_head(rows):
    width = rows.shape[1]
    return jnp.concatenate(
        [jnp.broadcast_to(rows[h : h + 1], (HEAD_DIM, width)) for h in range(HEADS)], axis=0
    )


def head_sums(values):
    return jnp.concatenate(
        [
            jnp.sum(values[h * HEAD_DIM : (h + 1) * HEAD_DIM], axis=0, keepdims=True)
            for h in range(HEADS)
        ],
        axis=0,
    )


def weight_and_slope(pre2):
    log = jnp.log2(1.0 + jnp.exp2(pre2))
    return jnp.exp2(0.2 * pre2 + 0.8 * log), 1.0 - 0.8 * jnp.exp2(-log)


def prepare(
    x_dst_ref, weight_ref, att_src_ref, att_dst_ref, grad_ref, mask_ref,
    proj_ref, grad_t_ref, mask_t_ref, spread_ref, self_ref, slope_ref, pair_ref,
):
    weight_t = weight_ref[...].astype(F32).T.astype(BF16)
    proj = mm(weight_t, x_dst_ref[...], NT).astype(BF16)
    proj_ref[...] = proj
    grad_t = grad_ref[...].astype(F32).T
    grad_t_ref[...] = grad_t.astype(BF16)
    parts = split3(head_rows(att_dst_ref[...])) + split3(head_rows(att_src_ref[...]))
    scores = mm(jnp.concatenate(parts, axis=0), proj)
    score_d = (scores[0:8] + scores[8:16]) + scores[16:24]
    score_own = (scores[24:32] + scores[32:40]) + scores[40:48]
    kind = lax.broadcasted_iota(jnp.int32, (SPREAD - HEADS, HEADS * BLK), 0)
    lane_head = lax.broadcasted_iota(jnp.int32, (SPREAD - HEADS, HEADS * BLK), 1) // BLK
    ones = jnp.where(kind % HEADS == lane_head, 1.0, 0.0)
    for r in range(spread_ref.shape[0]):
        line = jnp.concatenate(
            [score_d[h : h + 1, r * BLK : (r + 1) * BLK] for h in range(HEADS)], axis=1
        ) * LOG2E
        parts = [p.astype(F32) for p in split3(line)]
        rest = jnp.zeros((HEADS - len(parts), HEADS * BLK), F32)
        spread_ref[r] = jnp.concatenate([ones, *parts, rest], axis=0).astype(BF16)
    weight_self, slope_self = weight_and_slope((score_d + score_own) * LOG2E)
    self_ref[...] = weight_self
    slope_ref[...] = slope_self
    pair_ref[...] = head_sums(grad_t * proj.astype(F32))

    def turn(b, carry):
        mask_t_ref[b] = mask_ref[b].astype(F32).T
        return carry

    lax.fori_loop(0, mask_ref.shape[0], turn, 0)


def edges(
    rows_ref, cols_ref, place_ref,
    x_own_ref, x_other_ref, x_dst_ref, weight_ref, att_src_ref, att_src_col_ref, att_dst_col_ref,
    proj_ref, grad_t_ref, mask_t_ref, spread_ref, self_ref, slope_ref, pair_ref,
    grad_dst_ref, keep_ref, send_ref,
    proj_src, tiles, acc, scaled, scaled_c, own, grad_src_ref, grad_weight_ref, rows_out, score_cols, att_wide, x_all,
):
    slots = mask_t_ref.shape[0]
    dest_blocks = acc.shape[0]
    ext = acc.shape[2]
    weight = weight_ref[...]
    weight_t = weight.astype(F32).T.astype(BF16)
    att_rows = jnp.concatenate(split3(head_rows(att_src_ref[...])), axis=0)
    acc[...] = jnp.zeros(acc.shape, F32)
    grad_src_ref[...] = jnp.zeros(grad_src_ref.shape, grad_src_ref.dtype)
    ones = jnp.ones((ext - HEAD_DIM, BLK), BF16)

    att_wide[...] = jnp.broadcast_to(att_src_col_ref[...], att_wide.shape)

    core = place_ref[0] % 2
    half = x_own_ref.shape[0]
    x_all[0:half] = x_own_ref[...]
    x_all[half : 2 * half] = x_other_ref[...]

    def block(b):
        return pl.ds(pl.multiple_of(cols_ref[b] * BLK, BLK), BLK)

    def sources(b):
        col = cols_ref[b]
        place = (col % 2 + core) % 2 * half + col // 2 * BLK
        return x_all[pl.ds(pl.multiple_of(place, BLK), BLK), :]

    def project(step, carry):
        b = 2 * step
        pair = jnp.concatenate([sources(b), sources(b + 1)], axis=0)
        proj = mm(weight_t, pair, NT).astype(BF16)
        scores = mm(att_rows, proj)
        parts = split3(((scores[0:8] + scores[8:16]) + scores[16:24]) * LOG2E)
        tail = lax.broadcasted_iota(jnp.int32, (HEADS, 2 * BLK), 0)
        tail = jnp.where(tail < len(parts), 1.0, 0.0)
        cols = jnp.concatenate([*(p.astype(F32) for p in parts), tail], axis=0).T.astype(BF16)
        for k in range(2):
            proj_src[b + k] = proj[:, k * BLK : (k + 1) * BLK]
            score_cols[b + k] = cols[k * BLK : (k + 1) * BLK]
        return carry

    lax.fori_loop(0, slots // 2, project, 0, unroll=1)

    def forward(b, carry):
        row = rows_ref[b]
        proj = proj_src[b]
        cols = score_cols[b]
        mask = mask_t_ref[b]
        colsf = (cols[:,0:8].astype(F32)+cols[:,8:16].astype(F32))+cols[:,16:24].astype(F32)
        srow = (spread_ref[row,24:32].astype(F32)).sum(axis=0,keepdims=True)
        for h in range(HEADS):
            lanes = slice(h * BLK, (h + 1) * BLK)
            weight_e, slope = weight_and_slope(jnp.broadcast_to(colsf[:, h:h+1],(BLK,BLK)) + srow[:, lanes])
            weight_e = weight_e * mask
            pair = jnp.concatenate(
                [weight_e.astype(BF16), (weight_e * slope).astype(BF16)], axis=1
            )
            tiles[b, h] = pair
            left = jnp.concatenate([proj[h * HEAD_DIM : (h + 1) * HEAD_DIM], ones], axis=0)
            acc[row, h] += mm(left, pair)
        return carry

    lax.fori_loop(0, slots, forward, 0, unroll=2)

    self_att_rows, self_grad_rows, grad_d_rows = [], [], []
    for r in range(dest_blocks):
        lanes = slice(r * BLK, (r + 1) * BLK)
        self_w = self_ref[:, lanes]
        selfs, grads, dsts = [], [], []
        for h in range(HEADS):
            feats = slice(h * HEAD_DIM, (h + 1) * HEAD_DIM)
            sums = acc[r, h]
            w_self = self_w[h : h + 1]
            inv = 1.0 / (sums[HEAD_DIM : HEAD_DIM + 1, :BLK] + w_self)
            numer = sums[:HEAD_DIM, :BLK] + w_self * proj_ref[feats, lanes].astype(F32)
            grad = grad_t_ref[feats, lanes].astype(F32)
            part = (grad * inv).astype(BF16)
            part_wide = part.astype(F32)
            centred = jnp.sum(grad * numer, axis=0, keepdims=True) * inv
            centred_part = jnp.sum(part_wide * numer, axis=0, keepdims=True) * inv
            grad_d = (
                jnp.sum(part_wide * sums[:HEAD_DIM, BLK:], axis=0, keepdims=True)
                - centred_part * sums[HEAD_DIM : HEAD_DIM + 1, BLK:]
            )
            att_self = w_self * inv
            grad_self = (
                att_self * (pair_ref[h : h + 1, lanes] - centred) * slope_ref[h : h + 1, lanes]
            )
            scaled[r, h, 0:HEAD_DIM] = part
            c_hi, c_lo = split2(centred_part)
            scaled_c[r, h, 0:1] = c_hi.astype(F32)
            scaled_c[r, h, 1:2] = c_lo.astype(F32)
            selfs.append(att_self)
            grads.append(grad_self)
            dsts.append(grad_d + grad_self)
        self_att_rows.append(jnp.concatenate(selfs, axis=0))
        self_grad_rows.append(jnp.concatenate(grads, axis=0))
        grad_d_rows.append(jnp.concatenate(dsts, axis=0))
    for r in range(dest_blocks):
        for h in range(HEADS):
            scaled[r, h, HEAD_DIM:ext] = jnp.concatenate(
                [scaled_c[r, h, 0:2], jnp.zeros((ext - HEAD_DIM - 2, BLK), F32)], axis=0
            ).astype(BF16)

    att_src_wide = att_wide[...]
    att_dst_wide = jnp.broadcast_to(att_dst_col_ref[...], att_wide.shape)
    grad_weight = jnp.zeros((WIDTH, IN), F32)
    att_sums = jnp.zeros((WIDTH, 32), F32)
    for r in range(dest_blocks):
        lanes = slice(r * BLK, (r + 1) * BLK)
        grad_proj = (
            per_head(self_att_rows[r]) * grad_t_ref[:, lanes].astype(F32)
            + per_head(self_grad_rows[r]) * att_src_wide
            + per_head(grad_d_rows[r]) * att_dst_wide
        ).astype(BF16)
        grad_dst_ref[lanes, :] = mm(weight, grad_proj).T
        grad_weight = grad_weight + mm(grad_proj, x_dst_ref[lanes, :])
        both = jnp.concatenate(split2(self_grad_rows[r]) + split2(grad_d_rows[r]), axis=0)
        att_sums = att_sums + mm(proj_ref[:, lanes], both, NT)
    grad_weight_ref[...] = grad_weight
    own[...] = att_sums

    def back(b):
        row = rows_ref[b]
        proj = proj_src[b]
        feats, grads = [], []
        for h in range(HEADS):
            pair = tiles[b, h]
            stack = jnp.concatenate([pair[:, :BLK], pair[:, BLK:]], axis=0)
            out = mm(scaled[row, h], stack, NT)
            feats.append(out[:HEAD_DIM, :BLK])
            proj_h = proj[h * HEAD_DIM : (h + 1) * HEAD_DIM].astype(F32)
            grads.append(
                jnp.sum(proj_h * out[:HEAD_DIM, BLK:], axis=0, keepdims=True)
                - (out[HEAD_DIM : HEAD_DIM + 1, BLK:] + out[HEAD_DIM + 1 : HEAD_DIM + 2, BLK:])
            )
        grad_s = jnp.concatenate(grads, axis=0)
        grad_proj = jnp.concatenate(feats, axis=0) + per_head(grad_s) * att_wide[...]
        return proj, grad_s, grad_proj.astype(BF16)

    def backward(step, carry):
        b = 2 * step
        projs, grads, parts = zip(back(b), back(b + 1))
        grad_proj = jnp.concatenate(parts, axis=1)
        into = mm(weight, grad_proj)
        x_pair = jnp.concatenate([sources(b), sources(b + 1)], axis=0)
        grad_weight_ref[...] += mm(grad_proj, x_pair)
        grad_s = jnp.concatenate(split2(jnp.concatenate(grads, axis=1)), axis=0)
        own[:, 0:16] += mm(jnp.concatenate(projs, axis=1), grad_s, NT)
        for k in range(2):
            grad_src_ref[block(b + k), :] += into[:, k * BLK : (k + 1) * BLK].T
        return carry

    lax.fori_loop(0, slots // 2, backward, 0, unroll=2)

    sums = own[...]
    head = lax.broadcasted_iota(jnp.int32, (WIDTH, HEADS), 1)
    feat = lax.broadcasted_iota(jnp.int32, (WIDTH, HEADS), 0) // HEAD_DIM
    pick = head == feat
    src = jnp.where(pick, sums[:, 0:8] + sums[:, 8:16], 0.0)
    dst = jnp.where(pick, sums[:, 16:24] + sums[:, 24:32], 0.0)
    att_rows8 = [
        jnp.sum(part[f : f + LANES].T, axis=0, keepdims=True)
        for part in (src, dst)
        for f in range(0, WIDTH, LANES)
    ]
    att8 = jnp.concatenate(att_rows8, axis=0)
    for f in range(0, WIDTH, LANES):
        rows_out[f : f + LANES, :] = grad_weight_ref[f : f + LANES, :].T

    units = send_ref.shape[0]
    share = WIDTH // (2 * units)

    def pack(u, carry):
        for other, out in ((0, keep_ref), (1, send_ref)):
            panel = 2 * u + (core + other) % 2
            start = pl.multiple_of(panel * BLK, BLK)
            w_start = pl.multiple_of(panel * share, share)
            unit = jnp.concatenate(
                [
                    grad_src_ref[pl.ds(start, BLK), :],
                    rows_out[pl.ds(w_start, share), :],
                    jnp.where(panel == 0, att8, 0.0),
                ],
                axis=0,
            )
            out[u] = unit.astype(out.dtype)
        return carry

    lax.fori_loop(0, units, pack, 0)


def unpack(small_ref, grad_weight_ref, att_src_ref, att_dst_ref):
    panels = small_ref.shape[0]
    share = WIDTH // panels
    per = IN // share
    for p in range(panels):
        rows, lanes = p % per * share, p // per * LANES
        grad_weight_ref[rows : rows + share, lanes : lanes + LANES] = small_ref[p, 0:share].astype(F32)
    att = small_ref[0, share : share + 2 * WIDTH // LANES].astype(F32)
    pieces = WIDTH // LANES
    for k, out in enumerate((att_src_ref, att_dst_ref)):
        for q in range(pieces):
            line = att[k * pieces + q : k * pieces + q + 1]
            out[2 * q : 2 * q + 1, :] = line[:, :HEAD_DIM]
            out[2 * q + 1 : 2 * q + 2, :] = line[:, HEAD_DIM:]


def prep(x_dst, weight, att_src, att_dst, grad_out, block_masks):
    slots = block_masks.shape[0]
    dest = x_dst.shape[0]
    dest_blocks = dest // BLK
    att_src_row, att_dst_row = att_src.reshape(1, WIDTH), att_dst.reshape(1, WIDTH)
    params = pltpu.CompilerParams(vmem_limit_bytes=VMEM_BYTES)
    rows8 = jax.ShapeDtypeStruct((HEADS, dest), F32)
    return pl.pallas_call(
        prepare,
        out_shape=[
            jax.ShapeDtypeStruct((WIDTH, dest), BF16),
            jax.ShapeDtypeStruct((WIDTH, dest), BF16),
            jax.ShapeDtypeStruct((slots, BLK, BLK), F32),
            jax.ShapeDtypeStruct((dest_blocks, SPREAD, HEADS * BLK), BF16),
            rows8, rows8, rows8,
        ],
        compiler_params=params,
        cost_estimate=pl.CostEstimate(flops=2 * dest * IN * WIDTH, bytes_accessed=6 << 20, transcendentals=0),
        name="prepare",
    )(x_dst, weight, att_src_row, att_dst_row, grad_out, block_masks)


def local(x_own, x_other, x_dst, weight, att_src, att_dst, block_rows, block_cols, place, prepared):
    proj, grad_t, mask_t, spread, self_w, slope, pair = prepared
    slots = mask_t.shape[0]
    dest = x_dst.shape[0]
    dest_blocks = dest // BLK
    sources = 2 * x_own.shape[0]
    panels = sources // BLK
    att_src_row = att_src.reshape(1, WIDTH)
    att_src_col, att_dst_col = att_src.reshape(WIDTH, 1), att_dst.reshape(WIDTH, 1)
    params = pltpu.CompilerParams(vmem_limit_bytes=VMEM_BYTES)
    ext = 80
    operands = (
        x_own, x_other, x_dst, weight, att_src_row, att_src_col, att_dst_col,
        proj, grad_t, mask_t, spread, self_w, slope, pair,
    )
    units = panels // 2
    share = WIDTH // panels
    unit_rows = BLK + share + 8
    outs = [
        jax.ShapeDtypeStruct((dest, IN), F32),
        jax.ShapeDtypeStruct((units, unit_rows, LANES), F32),
        jax.ShapeDtypeStruct((units, unit_rows, LANES), BF16),
    ]
    return pl.pallas_call(
        edges,
        out_shape=outs,
        in_specs=[pl.BlockSpec(memory_space=pltpu.SMEM)] * 3
        + [pl.BlockSpec(memory_space=pltpu.VMEM)] * len(operands),
        out_specs=[pl.BlockSpec(memory_space=pltpu.VMEM)] * len(outs),
        scratch_shapes=[
            pltpu.VMEM((slots, WIDTH, BLK), BF16),
            pltpu.VMEM((slots, HEADS, BLK, 2 * BLK), BF16),
            pltpu.VMEM((dest_blocks, HEADS, ext, 2 * BLK), F32),
            pltpu.VMEM((dest_blocks, HEADS, ext, BLK), BF16),
            pltpu.VMEM((dest_blocks, HEADS, 8, BLK), F32),
            pltpu.VMEM((WIDTH, 32), F32),
            pltpu.VMEM((sources, IN), F32),
            pltpu.VMEM((WIDTH, IN), F32),
            pltpu.VMEM((WIDTH, IN), F32),
            pltpu.VMEM((slots, BLK, SPREAD), BF16),
            pltpu.VMEM((WIDTH, LANES), F32),
            pltpu.VMEM((sources, IN), BF16),
        ],
        compiler_params=params,
        cost_estimate=pl.CostEstimate(flops=4 << 30, bytes_accessed=12 << 20, transcendentals=8 << 20),
        name="edges",
    )(block_rows, block_cols, place, *operands)


def shards(
    x_src, x_dst, weight, att_src, att_dst, grad_out, block_rows, block_cols, block_masks, block_counts
):
    panels = lax.axis_size("panel")
    units = panels // 2
    share = WIDTH // panels
    same_core = [[p for p in range(panels) if p % 2 == core] for core in range(2)]
    siblings = [(p, p ^ 1) for p in range(panels)]

    def spread(values, axis, count, groups=None):
        return lax.all_to_all(
            jnp.broadcast_to(values[None], (count, *values.shape)), axis, 0, 0, axis_index_groups=groups
        )

    x_own = spread(x_src, "panel", units, same_core).reshape(-1, IN)
    prepared = prep(x_dst, weight, att_src, att_dst, grad_out, block_masks)
    x_own, prepared = lax.optimization_barrier((x_own, prepared))
    x_other = lax.ppermute(x_own, "panel", siblings)
    place = lax.axis_index("panel").reshape(1)
    grad_dst, keep, send = local(
        x_own, x_other, x_dst, weight, att_src, att_dst, block_rows, block_cols, place, prepared
    )
    half = (keep + lax.ppermute(send, "panel", siblings).astype(F32)).astype(BF16)
    got = lax.all_to_all(half, "panel", 0, 0, axis_index_groups=same_core)
    unit = got.astype(F32).sum(axis=0).astype(BF16)
    reps = lax.axis_size("rep")
    part, small = unit[:BLK], unit[BLK:]
    bit = 1
    while bit < reps:
        other = lax.ppermute(part, "rep", [(i, i ^ bit) for i in range(reps)])
        grad_src = part.astype(F32) + other.astype(F32)
        part = grad_src.astype(BF16)
        bit *= 2
    small = spread(small, "rep", reps).astype(F32).sum(axis=0).astype(BF16)
    small = spread(small, "panel", panels)
    grad_weight, grad_att_src, grad_att_dst = pl.pallas_call(
        unpack,
        out_shape=[
            jax.ShapeDtypeStruct((IN, WIDTH), F32),
            jax.ShapeDtypeStruct((HEADS, HEAD_DIM), F32),
            jax.ShapeDtypeStruct((HEADS, HEAD_DIM), F32),
        ],
        name="unpack",
    )(small)
    return grad_src, grad_dst, grad_weight, grad_att_src, grad_att_dst


def solution(mesh):
    return jax.shard_map(
        shards,
        mesh=mesh,
        in_specs=(
            P("panel", None),
            P(("panel", "rep"), None),
            P(),
            P(),
            P(),
            P(("panel", "rep"), None),
            P(("panel", "rep")),
            P(("panel", "rep")),
            P(("panel", "rep"), None, None),
            P(("panel", "rep")),
        ),
        out_specs=(P("panel", None), P(("panel", "rep"), None), P(), P(), P()),
        check_vma=False,
    )
```

time: 682 us -> 117 us (0.17); the launches traced: 674 us -> 116 us
  waiting for transfers between devices: 438 us -> 25.4 us
  matrix products: 70.2 us -> 0 us
  blocking collectives: 80.4 us -> 21.9 us
  local copies, waits for them, and re-layouts: 43.3 us -> 11.5 us
  starting transfers between devices: 0.16 us -> 29.5 us
  Pallas kernels: 0 us -> 26.2 us
  other arithmetic: 26.5 us -> 0.91 us
  between operations: 15.2 us -> 0.82 us
    psum x2 -> x0, waiting for transfers between devices: 261 us -> none  [the longest x1 255 us: shards(): lax.psum((weight_part, att_src_part, att_dst_part), ('panel', 'rep'))]
    reduce_scatter x1 -> x0, waiting for transfers between devices: 119 us -> none  [shards(): lax.psum_scatter(source_flat, 'panel', scatter_dimension=0, tiled=True)]
    psum x1 -> x0, blocking collectives: 80.4 us -> none  [shards(): lax.psum((weight_part, att_src_part, att_dst_part), ('panel', 'rep'))]
    dot_general x24 -> x0, matrix products: 70.2 us -> none  [the longest x1 15.5 us: backward_group(): jnp.einsum('gihk,gjhk->ghij', cotan_rows, source_rows, preferred_element_...]
    all_gather x1 -> x0, waiting for transfers between devices: 58.5 us -> none  [shards(): proj_all = lax.all_gather(proj_own, 'panel', axis=0, tiled=True)]
    pallas_call x0 -> x3, Pallas kernels: none -> 26.2 us  [the longest x1 22.2 us: local(): pl.pallas_call(edges, out_shape=outs, in_specs=[pl.BlockSpec(memory_space...]
    another operation x4 -> x0, local copies, waits for them, and re-layouts: 22.5 us -> none  [the longest x2 20.2 us: shards(): source_feats.reshape(source_blocks, block_size, num_heads, head_dim)]
    all_to_all x0 -> x1, blocking collectives: none -> 21.9 us  [shards(): got = lax.all_to_all(half, 'panel', 0, 0, axis_index_groups=same_core)]
  transfers between devices with their start and end apart: 4 -> 8, of which waited for: 4 -> 6; matrix products, arithmetic and copies ran while one was open for 3% -> 2% of each run, Pallas kernels for 0% -> 2%
where the time goes in v1:
time: 117 us; the launch traced here: 116 us
  starting transfers between devices  29.5 us (25%)
  Pallas kernels  26.2 us (22%)
  waiting for transfers between devices  25.4 us (22%)
  blocking collectives  21.9 us (19%)
  local copies, waits for them, and re-layouts  11.5 us (10%)
    pallas_call x1, Pallas kernels, local(): pl.pallas_call(edges, out_shape=outs, in_specs=[pl.BlockSpec(memory_space...  22.2 us
    all_to_all x1, blocking collectives, shards(): got = lax.all_to_all(half, 'panel', 0, 0, axis_index_groups=same_core)  21.9 us
    all_to_all x3, starting transfers between devices, spread(): lax.all_to_all(jnp.broadcast_to(values[None], (count, *values.shape)), ax...  21.3 us
    all_to_all x3, waiting for transfers between devices, spread(): lax.all_to_all(jnp.broadcast_to(values[None], (count, *values.shape)), ax...  19.4 us
    unnamed x34, local copies, waits for them, and re-layouts  7.85 us
    ppermute x3, starting transfers between devices, shards(): other = lax.ppermute(part, 'rep', [(i, i ^ bit) for i in range(reps)])  5.35 us
    ppermute x3, waiting for transfers between devices, shards(): other = lax.ppermute(part, 'rep', [(i, i ^ bit) for i in range(reps)])  3.25 us
    broadcast_in_dim x3, local copies, waits for them, and re-layouts, spread(): jnp.broadcast_to(values[None], (count, *values.shape))  3.11 us
  transfers between devices with their start and end apart: 8, of which 6 were waited for; matrix products, arithmetic and copies ran while one was open for 2% of the time, Pallas kernels for 2%

profile of v1, /device:TPU:1, one launch (start us, length us, event | category | flops | bytes accessed | tf_op | source)
XLA Modules:
  0.0 116.2 jit_solution(11987308012021240421)
XLA Ops:
  0.7 1.8 %broadcast_in_dim.6 = bf16[16,128,128]{2,1,0:T(8,128)(2,1)} broadcast(bf16[128,128]{1,0:T(8,128)(2,1)} %param.10), dimensions={1,2} | broadcast | bytes 557056 | tf_op jit(solution)/shard_map/broadcast_in_dim | solution.py:394
  2.5 10.1 %all-to-all-start = ((bf16[16,128,128]{2,1,0:T(8,128)(2,1)}), bf16[16,128,128]{2,1,0:T(8,128)(2,1)S(1)}, u32[]{:S(2)}, u32[]{:S(2)}) async-start(bf16[16,128,128]{2,1,0:T(8,128)(2,1)} %broadcast_in_dim.6), calls=%async_computation | async-start | bytes 1048576 | tf_op jit(solution)/shard_map/all_to_all | solution.py:393
  12.8 0.9 copy-done.2
  13.7 0.9 copy-done.4
  14.6 2.3 %prepare.1 = (bf16[512,512]{1,0:T(8,128)(2,1)S(1)}, bf16[512,512]{1,0:T(8,128)(2,1)S(1)}, f32[16,128,128]{2,1,0:T(8,128)S(1)}, bf16[4,32,1024]{2,1,0:T(8,128)(2,...) custom-call(bf16[512,128]{1,0:T(8,128)(2,1)S(1)} %copy-done.2, ...), custom_call_target="tpu_custom_call" | custom-call | flops 67108864 | bytes 6291456 | tf_op jit(solution)/shard_map/prepare/pallas_call | solution.py:319
  17.7 0.8 copy-done.8
  19.2 9.0 %all-to-all-done = bf16[16,128,128]{2,1,0:T(8,128)(2,1)S(1)} async-done(((bf16[16,128,128]{2,1,0:T(8,128)(2,1)}), bf16[16,128,128]{2,1,0:T(8,128)(2,1)S(1)}, u32[]{:S(2)}, u32[]{:S(2)}) %all-to-all-start) | async-done | bytes 524320 | tf_op jit(solution)/shard_map/all_to_all | solution.py:393
  28.2 2.5 %collective-permute-start = (bf16[2048,128]{1,0:T(8,128)(2,1)S(1)}, bf16[2048,128]{1,0:T(8,128)(2,1)S(1)}, u32[]{:S(2)}, u32[]{:S(2)}) collective-permute-start(bf16[2048,128]{1,0:T(8,128)(2,1)S(1)} %bitcast.2), channel_id=1, source_target_pairs={{0,8},{8,0},{16,24},{24,16},{32,40},{40,32},{48,56},{56,48},{64,72... | collective-permute-start | bytes 1572872 | tf_op jit(solution)/shard_map/ppermute | solution.py:400
  31.1 1.1 collective-permute-done.x_other_ref
  32.3 1.0 copy-done.7
  33.3 1.0 copy-done.9
  34.3 0.9 copy-done.11
  35.3 22.2 %edges.1 = (f32[512,128]{1,0:T(8,128)}, f32[16,152,128]{2,1,0:T(8,128)S(1)}, bf16[16,152,128]{2,1,0:T(8,128)(2,1)S(1)}) custom-call(s32[16]{0:T(128)S(1)} %copy-done.12, s32[16]{0:T(128)S(1)} %copy-done.13, s32[1]{0:T(128)} %bitcast.place_ref, bf16[2048,128]{1,0:T(8,128)(2,1)S(1)} %bitcast.3, bf16[2048,128]{1,0:T(8,128)(2,1)S(1)} %collective-permute-done.x_other_ref, ...), custom_call_target="tpu_custom_call" | custom-call | flops 4294967296 | bytes 12582912 | tf_op jit(solution)/shard_map/edges/pallas_call | solution.py:357
  57.8 1.7 %collective-permute-done.1 = bf16[16,152,128]{2,1,0:T(8,128)(2,1)S(1)} collective-permute-done((bf16[16,152,128]{2,1,0:T(8,128)(2,1)S(1)}, bf16[16,152,128]{2,1,0:T(8,128)(2,1)S(1)}, u32[]{:S(2)}, u32[]{:S(2)}) %collective-permute-start.1) | collective-permute-done | bytes 622624 | tf_op jit(solution)/shard_map/ppermute | solution.py:405
  59.7 21.9 %all_to_all.20 = bf16[16,152,128]{2,1,0:T(8,128)(2,1)S(1)} all-to-all(bf16[16,152,128]{2,1,0:T(8,128)(2,1)S(1)} %add_convert_fusion), channel_id=1, replica_groups={{0,16,32,48,64,80,96,112,128,144,160,176,192,208,224,240},{8,24,40,56,7..., dimensions={0} | all-to-all | bytes 1245184 | tf_op jit(solution)/shard_map/all_to_all | solution.py:406
  81.7 2.7 %collective-permute-start.2 = (bf16[128,128]{1,0:T(8,128)(2,1)S(1)}, bf16[128,128]{1,0:T(8,128)(2,1)S(1)}, u32[]{:S(2)}, u32[]{:S(2)}) collective-permute-start(bf16[128,128]{1,0:T(8,128)(2,1)S(1)} %slice.8), channel_id=1, source_target_pairs={{0,1},{1,0},{2,3},{3,2},{4,5},{5,4},{6,7},{7,6},{8,9},{9,8},{10,11... | collective-permute-start | bytes 98312 | tf_op jit(solution)/shard_map/ppermute | solution.py:412
  85.0 4.1 %all-to-all-start.2 = ((bf16[8,24,128]{2,1,0:T(8,128)(2,1)}), bf16[8,24,128]{2,1,0:T(8,128)(2,1)S(1)}, u32[]{:S(2)}, u32[]{:S(2)}) async-start(bf16[8,24,128]{2,1,0:T(8,128)(2,1)} %broadcast_in_dim.7), calls=%async_computation.2 | async-start | bytes 98304 | tf_op jit(solution)/shard_map/all_to_all | solution.py:393
  89.2 1.5 %collective-permute-start.3 = (bf16[128,128]{1,0:T(8,128)(2,1)S(1)}, bf16[128,128]{1,0:T(8,128)(2,1)S(1)}, u32[]{:S(2)}, u32[]{:S(2)}) collective-permute-start(bf16[128,128]{1,0:T(8,128)(2,1)S(1)} %add_convert_fusion.2), channel_id=1, source_target_pairs={{0,2},{1,3},{2,0},{3,1},{4,6},{5,7},{6,4},{7,5},{8,10},{9,11},{10,... | collective-permute-start | bytes 98312 | tf_op jit(solution)/shard_map/ppermute | solution.py:412
  90.7 5.0 %all-to-all-done.2 = bf16[8,24,128]{2,1,0:T(8,128)(2,1)S(1)} async-done(((bf16[8,24,128]{2,1,0:T(8,128)(2,1)}), bf16[8,24,128]{2,1,0:T(8,128)(2,1)S(1)}, u32[]{:S(2)}, u32[]{:S(2)}) %all-to-all-start.2) | async-done | bytes 49184 | tf_op jit(solution)/shard_map/all_to_all | solution.py:393
  96.4 7.1 %all-to-all-start.3 = ((bf16[32,24,128]{2,1,0:T(8,128)(2,1)}), bf16[32,24,128]{2,1,0:T(8,128)(2,1)S(1)}, u32[]{:S(2)}, u32[]{:S(2)}) async-start(bf16[32,24,128]{2,1,0:T(8,128)(2,1)} %broadcast_in_dim.8), calls=%async_computation.3 | async-start | bytes 393216 | tf_op jit(solution)/shard_map/all_to_all | solution.py:393
  103.6 1.1 collective-permute-start.4
  104.7 3.2 %collective-permute-done.4 = bf16[128,128]{1,0:T(8,128)(2,1)S(1)} collective-permute-done((bf16[128,128]{1,0:T(8,128)(2,1)S(1)}, bf16[128,128]{1,0:T(8,128)(2,1)S(1)}, u32[]{:S(2)}, u32[]{:S(2)}) %collective-permute-start.4) | collective-permute-done | bytes 32800 | tf_op jit(solution)/shard_map/ppermute | solution.py:412
  108.6 5.3 %all-to-all-done.3.small_ref = bf16[32,24,128]{2,1,0:T(8,128)(2,1)S(1)} async-done(((bf16[32,24,128]{2,1,0:T(8,128)(2,1)}), bf16[32,24,128]{2,1,0:T(8,128)(2,1)S(1)}, u32[]{:S(2)}, u32[]{:S(2)}) %all-to-all-start.3) | async-done | bytes 196640 | tf_op jit(solution)/shard_map/all_to_all | solution.py:393
  114.6 1.7 %unpack.1 = (f32[128,512]{1,0:T(8,128)}, f32[8,64]{1,0:T(8,128)}, f32[8,64]{1,0:T(8,128)}) custom-call(bf16[32,24,128]{2,1,0:T(8,128)(2,1)} %copy-done.14), custom_call_target="tpu_custom_call" | custom-call | tf_op jit(solution)/shard_map/unpack/pallas_call | solution.py:418
  (45 shorter events, 5.4 us)
Async XLA Ops:
  0.6 12.0 %copy-start.15 = (f32[8,64]{1,0:T(8,128)S(1)}, f32[8,64]{1,0:T(8,128)}, u32[]{:S(2)}) copy-start(f32[8,64]{1,0:T(8,128)} %param.13) | copy-start | bytes 6148
  0.6 12.1 %copy-start.16 = (f32[8,64]{1,0:T(8,128)S(1)}, f32[8,64]{1,0:T(8,128)}, u32[]{:S(2)}) copy-start(f32[8,64]{1,0:T(8,128)} %param.14) | copy-start | bytes 6148
  0.7 12.1 %copy-start = (s32[16,128,128]{2,1,0:T(8,128)S(1)}, s32[16,128,128]{2,1,0:T(8,128)}, u32[]{:S(2)}) copy-start(s32[16,128,128]{2,1,0:T(8,128)} %mask_ref.1) | copy-start | bytes 3145732
  0.7 12.1 %copy-start.1 = (bf16[512,512]{1,0:T(8,128)(2,1)S(1)}, bf16[512,512]{1,0:T(8,128)(2,1)}, u32[]{:S(2)}) copy-start(bf16[512,512]{1,0:T(8,128)(2,1)} %grad_ref.1) | copy-start | bytes 1572868
  2.5 25.8 %all-to-all-start = ((bf16[16,128,128]{2,1,0:T(8,128)(2,1)}), bf16[16,128,128]{2,1,0:T(8,128)(2,1)S(1)}, u32[]{:S(2)}, u32[]{:S(2)}) async-start(bf16[16,128,128]{2,1,0:T(8,128)(2,1)} %broadcast_in_dim.6), calls=%async_computation | async-start | bytes 1048576 | tf_op jit(solution)/shard_map/all_to_all | solution.py:393
  12.6 19.6 %copy-start.12 = (s32[16]{0:T(128)S(1)}, s32[16]{0:T(128)}, u32[]{:S(2)}) copy-start(s32[16]{0:T(128)} %rows_ref.1) | copy-start | bytes 196
  12.6 19.6 %copy-start.13 = (s32[16]{0:T(128)S(1)}, s32[16]{0:T(128)}, u32[]{:S(2)}) copy-start(s32[16]{0:T(128)} %cols_ref.1) | copy-start | bytes 196
  12.8 0.9 copy-start.2
  13.7 0.9 copy-start.4
  14.6 17.6 %copy-start.3 = (bf16[512,128]{1,0:T(8,128)(2,1)S(1)}, bf16[512,128]{1,0:T(8,128)(2,1)}, u32[]{:S(2)}) copy-start(bf16[512,128]{1,0:T(8,128)(2,1)} %x_dst_ref.3) | copy-start | bytes 393220
  14.6 17.7 %copy-start.5 = (bf16[128,512]{1,0:T(8,128)(2,1)S(1)}, bf16[128,512]{1,0:T(8,128)(2,1)}, u32[]{:S(2)}) copy-start(bf16[128,512]{1,0:T(8,128)(2,1)} %weight_ref.3) | copy-start | bytes 393220
  16.9 0.8 copy-start.6
  17.7 0.8 copy-start.8
  18.5 0.7 copy-start.10
  28.2 4.0 %collective-permute-start = (bf16[2048,128]{1,0:T(8,128)(2,1)S(1)}, bf16[2048,128]{1,0:T(8,128)(2,1)S(1)}, u32[]{:S(2)}, u32[]{:S(2)}) collective-permute-start(bf16[2048,128]{1,0:T(8,128)(2,1)S(1)} %bitcast.2), channel_id=1, source_target_pairs={{0,8},{8,0},{16,24},{24,16},{32,40},{40,32},{48,56},{56,48},{64,72... | collective-permute-start | bytes 1572872 | tf_op jit(solution)/shard_map/ppermute | solution.py:400
  32.3 1.0 copy-start.7
  33.3 1.0 copy-start.9
  34.3 0.9 copy-start.11
  57.5 2.1 %collective-permute-start.1 = (bf16[16,152,128]{2,1,0:T(8,128)(2,1)S(1)}, bf16[16,152,128]{2,1,0:T(8,128)(2,1)S(1)}, u32[]{:S(2)}, u32[]{:S(2)}) collective-permute-start(bf16[16,152,128]{2,1,0:T(8,128)(2,1)S(1)} %get-tuple-element.42), channel_id=1, source_target_pairs={{0,8},{8,0},{16,24},{24,16},{32,40},{40,32},{48,56},{56,48},{64,72... | collective-permute-start | bytes 1867784 | tf_op jit(solution)/shard_map/ppermute | solution.py:405
  81.7 7.4 %collective-permute-start.2 = (bf16[128,128]{1,0:T(8,128)(2,1)S(1)}, bf16[128,128]{1,0:T(8,128)(2,1)S(1)}, u32[]{:S(2)}, u32[]{:S(2)}) collective-permute-start(bf16[128,128]{1,0:T(8,128)(2,1)S(1)} %slice.8), channel_id=1, source_target_pairs={{0,1},{1,0},{2,3},{3,2},{4,5},{5,4},{6,7},{7,6},{8,9},{9,8},{10,11... | collective-permute-start | bytes 98312 | tf_op jit(solution)/shard_map/ppermute | solution.py:412
  85.0 10.7 %all-to-all-start.2 = ((bf16[8,24,128]{2,1,0:T(8,128)(2,1)}), bf16[8,24,128]{2,1,0:T(8,128)(2,1)S(1)}, u32[]{:S(2)}, u32[]{:S(2)}) async-start(bf16[8,24,128]{2,1,0:T(8,128)(2,1)} %broadcast_in_dim.7), calls=%async_computation.2 | async-start | bytes 98304 | tf_op jit(solution)/shard_map/all_to_all | solution.py:393
  89.2 14.4 %collective-permute-start.3 = (bf16[128,128]{1,0:T(8,128)(2,1)S(1)}, bf16[128,128]{1,0:T(8,128)(2,1)S(1)}, u32[]{:S(2)}, u32[]{:S(2)}) collective-permute-start(bf16[128,128]{1,0:T(8,128)(2,1)S(1)} %add_convert_fusion.2), channel_id=1, source_target_pairs={{0,2},{1,3},{2,0},{3,1},{4,6},{5,7},{6,4},{7,5},{8,10},{9,11},{10,... | collective-permute-start | bytes 98312 | tf_op jit(solution)/shard_map/ppermute | solution.py:412
  96.4 17.5 %all-to-all-start.3 = ((bf16[32,24,128]{2,1,0:T(8,128)(2,1)}), bf16[32,24,128]{2,1,0:T(8,128)(2,1)S(1)}, u32[]{:S(2)}, u32[]{:S(2)}) async-start(bf16[32,24,128]{2,1,0:T(8,128)(2,1)} %broadcast_in_dim.8), calls=%async_computation.3 | async-start | bytes 393216 | tf_op jit(solution)/shard_map/all_to_all | solution.py:393
  103.6 4.4 %collective-permute-start.4 = (bf16[128,128]{1,0:T(8,128)(2,1)S(1)}, bf16[128,128]{1,0:T(8,128)(2,1)S(1)}, u32[]{:S(2)}, u32[]{:S(2)}) collective-permute-start(bf16[128,128]{1,0:T(8,128)(2,1)S(1)} %add_convert_fusion.1), channel_id=1, source_target_pairs={{0,4},{1,5},{2,6},{3,7},{4,0},{5,1},{6,2},{7,3},{8,12},{9,13},{10,... | collective-permute-start | bytes 98312 | tf_op jit(solution)/shard_map/ppermute | solution.py:412
  (1 other events, 0.7 us)

commit v2 on v1

--- a/solution.py
+++ b/solution.py
@@ -10,7 +10,6 @@
 LANES = 128
 F32, BF16 = jnp.float32, jnp.bfloat16
 VMEM_BYTES = 40 << 20
-SPREAD = 32
 
 NN = (((1,), (0,)), ((), ()))
 NT = (((1,), (1,)), ((), ()))
@@ -63,7 +62,7 @@
 
 def prepare(
     x_dst_ref, weight_ref, att_src_ref, att_dst_ref, grad_ref, mask_ref,
-    proj_ref, grad_t_ref, mask_t_ref, spread_ref, self_ref, slope_ref, pair_ref,
+    proj_ref, grad_t_ref, mask_t_ref, score_ref, self_ref, slope_ref, pair_ref,
 ):
     weight_t = weight_ref[...].astype(F32).T.astype(BF16)
     proj = mm(weight_t, x_dst_ref[...], NT).astype(BF16)
@@ -74,16 +73,8 @@
     scores = mm(jnp.concatenate(parts, axis=0), proj)
     score_d = (scores[0:8] + scores[8:16]) + scores[16:24]
     score_own = (scores[24:32] + scores[32:40]) + scores[40:48]
-    kind = lax.broadcasted_iota(jnp.int32, (SPREAD - HEADS, HEADS * BLK), 0)
-    lane_head = lax.broadcasted_iota(jnp.int32, (SPREAD - HEADS, HEADS * BLK), 1) // BLK
-    ones = jnp.where(kind % HEADS == lane_head, 1.0, 0.0)
-    for r in range(spread_ref.shape[0]):
-        line = jnp.concatenate(
-            [score_d[h : h + 1, r * BLK : (r + 1) * BLK] for h in range(HEADS)], axis=1
-        ) * LOG2E
-        parts = [p.astype(F32) for p in split3(line)]
-        rest = jnp.zeros((HEADS - len(parts), HEADS * BLK), F32)
-        spread_ref[r] = jnp.concatenate([ones, *parts, rest], axis=0).astype(BF16)
+    for r in range(score_ref.shape[0]):
+        score_ref[r] = score_d[:, r * BLK : (r + 1) * BLK] * LOG2E
     weight_self, slope_self = weight_and_slope((score_d + score_own) * LOG2E)
     self_ref[...] = weight_self
     slope_ref[...] = slope_self
@@ -99,7 +90,7 @@
 def edges(
     rows_ref, cols_ref, place_ref,
     x_own_ref, x_other_ref, x_dst_ref, weight_ref, att_src_ref, att_src_col_ref, att_dst_col_ref,
-    proj_ref, grad_t_ref, mask_t_ref, spread_ref, self_ref, slope_ref, pair_ref,
+    proj_ref, grad_t_ref, mask_t_ref, score_ref, self_ref, slope_ref, pair_ref,
     grad_dst_ref, keep_ref, send_ref,
     proj_src, tiles, acc, scaled, scaled_c, own, grad_src_ref, grad_weight_ref, rows_out, score_cols, att_wide, x_all,
 ):
@@ -128,32 +119,23 @@
         place = (col % 2 + core) % 2 * half + col // 2 * BLK
         return x_all[pl.ds(pl.multiple_of(place, BLK), BLK), :]
 
-    def project(step, carry):
-        b = 2 * step
-        pair = jnp.concatenate([sources(b), sources(b + 1)], axis=0)
-        proj = mm(weight_t, pair, NT).astype(BF16)
-        scores = mm(att_rows, proj)
-        parts = split3(((scores[0:8] + scores[8:16]) + scores[16:24]) * LOG2E)
-        tail = lax.broadcasted_iota(jnp.int32, (HEADS, 2 * BLK), 0)
-        tail = jnp.where(tail < len(parts), 1.0, 0.0)
-        cols = jnp.concatenate([*(p.astype(F32) for p in parts), tail], axis=0).T.astype(BF16)
-        for k in range(2):
-            proj_src[b + k] = proj[:, k * BLK : (k + 1) * BLK]
-            score_cols[b + k] = cols[k * BLK : (k + 1) * BLK]
-        return carry
-
-    lax.fori_loop(0, slots // 2, project, 0, unroll=1)
+    group = jnp.concatenate([sources(b) for b in range(slots)], axis=0)
+    projs = mm(weight_t, group, NT).astype(BF16)
+    scores = mm(att_rows, projs)
+    score_t = (((scores[0:8] + scores[8:16]) + scores[16:24]) * LOG2E).T
+    for b in range(slots):
+        proj_src[b] = projs[:, b * BLK : (b + 1) * BLK]
+        score_cols[b] = score_t[b * BLK : (b + 1) * BLK]
 
     def forward(b, carry):
         row = rows_ref[b]
         proj = proj_src[b]
         cols = score_cols[b]
         mask = mask_t_ref[b]
-        colsf = (cols[:,0:8].astype(F32)+cols[:,8:16].astype(F32))+cols[:,16:24].astype(F32)
-        srow = (spread_ref[row,24:32].astype(F32)).sum(axis=0,keepdims=True)
+        score_d = score_ref[row]
         for h in range(HEADS):
-            lanes = slice(h * BLK, (h + 1) * BLK)
-            weight_e, slope = weight_and_slope(jnp.broadcast_to(colsf[:, h:h+1],(BLK,BLK)) + srow[:, lanes])
+            pre2 = jnp.broadcast_to(cols[:, h : h + 1], (BLK, BLK)) + score_d[h : h + 1]
+            weight_e, slope = weight_and_slope(pre2)
             weight_e = weight_e * mask
             pair = jnp.concatenate(
                 [weight_e.astype(BF16), (weight_e * slope).astype(BF16)], axis=1
@@ -163,7 +145,7 @@
             acc[row, h] += mm(left, pair)
         return carry
 
-    lax.fori_loop(0, slots, forward, 0, unroll=2)
+    lax.fori_loop(0, slots, forward, 0, unroll=4)
 
     self_att_rows, self_grad_rows, grad_d_rows = [], [], []
     for r in range(dest_blocks):
@@ -254,7 +236,7 @@
             grad_src_ref[block(b + k), :] += into[:, k * BLK : (k + 1) * BLK].T
         return carry
 
-    lax.fori_loop(0, slots // 2, backward, 0, unroll=2)
+    lax.fori_loop(0, slots // 2, backward, 0, unroll=8)
 
     sums = own[...]
     head = lax.broadcasted_iota(jnp.int32, (WIDTH, HEADS), 1)
@@ -293,22 +275,6 @@
     lax.fori_loop(0, units, pack, 0)
 
 
-def unpack(small_ref, grad_weight_ref, att_src_ref, att_dst_ref):
-    panels = small_ref.shape[0]
-    share = WIDTH // panels
-    per = IN // share
-    for p in range(panels):
-        rows, lanes = p % per * share, p // per * LANES
-        grad_weight_ref[rows : rows + share, lanes : lanes + LANES] = small_ref[p, 0:share].astype(F32)
-    att = small_ref[0, share : share + 2 * WIDTH // LANES].astype(F32)
-    pieces = WIDTH // LANES
-    for k, out in enumerate((att_src_ref, att_dst_ref)):
-        for q in range(pieces):
-            line = att[k * pieces + q : k * pieces + q + 1]
-            out[2 * q : 2 * q + 1, :] = line[:, :HEAD_DIM]
-            out[2 * q + 1 : 2 * q + 2, :] = line[:, HEAD_DIM:]
-
-
 def prep(x_dst, weight, att_src, att_dst, grad_out, block_masks):
     slots = block_masks.shape[0]
     dest = x_dst.shape[0]
@@ -322,7 +288,7 @@
             jax.ShapeDtypeStruct((WIDTH, dest), BF16),
             jax.ShapeDtypeStruct((WIDTH, dest), BF16),
             jax.ShapeDtypeStruct((slots, BLK, BLK), F32),
-            jax.ShapeDtypeStruct((dest_blocks, SPREAD, HEADS * BLK), BF16),
+            jax.ShapeDtypeStruct((dest_blocks, HEADS, BLK), F32),
             rows8, rows8, rows8,
         ],
         compiler_params=params,
@@ -332,7 +298,7 @@
 
 
 def local(x_own, x_other, x_dst, weight, att_src, att_dst, block_rows, block_cols, place, prepared):
-    proj, grad_t, mask_t, spread, self_w, slope, pair = prepared
+    proj, grad_t, mask_t, score, self_w, slope, pair = prepared
     slots = mask_t.shape[0]
     dest = x_dst.shape[0]
     dest_blocks = dest // BLK
@@ -344,7 +310,7 @@
     ext = 80
     operands = (
         x_own, x_other, x_dst, weight, att_src_row, att_src_col, att_dst_col,
-        proj, grad_t, mask_t, spread, self_w, slope, pair,
+        proj, grad_t, mask_t, score, self_w, slope, pair,
     )
     units = panels // 2
     share = WIDTH // panels
@@ -370,7 +336,7 @@
             pltpu.VMEM((sources, IN), F32),
             pltpu.VMEM((WIDTH, IN), F32),
             pltpu.VMEM((WIDTH, IN), F32),
-            pltpu.VMEM((slots, BLK, SPREAD), BF16),
+            pltpu.VMEM((slots, BLK, HEADS), F32),
             pltpu.VMEM((WIDTH, LANES), F32),
             pltpu.VMEM((sources, IN), BF16),
         ],
@@ -396,7 +362,8 @@
 
     x_own = spread(x_src, "panel", units, same_core).reshape(-1, IN)
     prepared = prep(x_dst, weight, att_src, att_dst, grad_out, block_masks)
-    x_own, prepared = lax.optimization_barrier((x_own, prepared))
+    x_own, slope = lax.optimization_barrier((x_own, prepared[5]))
+    prepared = [*prepared[:5], slope, *prepared[6:]]
     x_other = lax.ppermute(x_own, "panel", siblings)
     place = lax.axis_index("panel").reshape(1)
     grad_dst, keep, send = local(
@@ -405,26 +372,12 @@
     half = (keep + lax.ppermute(send, "panel", siblings).astype(F32)).astype(BF16)
     got = lax.all_to_all(half, "panel", 0, 0, axis_index_groups=same_core)
     unit = got.astype(F32).sum(axis=0).astype(BF16)
-    reps = lax.axis_size("rep")
-    part, small = unit[:BLK], unit[BLK:]
-    bit = 1
-    while bit < reps:
-        other = lax.ppermute(part, "rep", [(i, i ^ bit) for i in range(reps)])
-        grad_src = part.astype(F32) + other.astype(F32)
-        part = grad_src.astype(BF16)
-        bit *= 2
-    small = spread(small, "rep", reps).astype(F32).sum(axis=0).astype(BF16)
-    small = spread(small, "panel", panels)
-    grad_weight, grad_att_src, grad_att_dst = pl.pallas_call(
-        unpack,
-        out_shape=[
-            jax.ShapeDtypeStruct((IN, WIDTH), F32),
-            jax.ShapeDtypeStruct((HEADS, HEAD_DIM), F32),
-            jax.ShapeDtypeStruct((HEADS, HEAD_DIM), F32),
-        ],
-        name="unpack",
-    )(small)
-    return grad_src, grad_dst, grad_weight, grad_att_src, grad_att_dst
+    total = spread(unit, "rep", lax.axis_size("rep")).astype(F32).sum(axis=0)
+    grad_src = total[:BLK]
+    small = spread(total[BLK:].astype(BF16), "panel", panels).astype(F32)
+    grad_weight = small[:, :share].reshape(WIDTH // LANES, IN, LANES).transpose(1, 0, 2).reshape(IN, WIDTH)
+    att = small[0, share:].reshape(2, HEADS, HEAD_DIM)
+    return grad_src, grad_dst, grad_weight, att[0], att[1]
 
 
 def solution(mesh):

time: 117 us -> 110 us (0.940)
  blocking collectives: 21.9 us -> 36.1 us
  starting transfers between devices: 29.5 us -> 19.8 us
  Pallas kernels: 26.2 us -> 19 us
  waiting for transfers between devices: 25.4 us -> 22.3 us
    all_to_all x0 -> x1, blocking collectives: none -> 14.1 us  [spread(): lax.all_to_all(jnp.broadcast_to(values[None], (count, *values.shape)), ax...]
    pallas_call x1, Pallas kernels: 22.2 us -> 16.7 us  [local(): pl.pallas_call(edges, out_shape=outs, in_specs=[pl.BlockSpec(memory_space...]
    ppermute x3 -> x0, starting transfers between devices: 5.35 us -> none  [shards(): other = lax.ppermute(part, 'rep', [(i, i ^ bit) for i in range(reps)])]
    all_to_all x3 -> x2, starting transfers between devices: 21.3 us -> 16.9 us  [spread(): lax.all_to_all(jnp.broadcast_to(values[None], (count, *values.shape)), ax...]
    ppermute x3 -> x0, waiting for transfers between devices: 3.25 us -> none  [shards(): other = lax.ppermute(part, 'rep', [(i, i ^ bit) for i in range(reps)])]
    pallas_call x1 -> x0, Pallas kernels: 1.66 us -> none  [shards(): pl.pallas_call(unpack, out_shape=[jax.ShapeDtypeStruct((IN, WIDTH), F32),...]
    unnamed x34 -> x29, local copies, waits for them, and re-layouts: 7.85 us -> 6.26 us
    squeeze x0 -> x2, local copies, waits for them, and re-layouts: none -> 1.34 us  [shards(): return (grad_src, grad_dst, grad_weight, att[0], att[1])]
  transfers between devices with their start and end apart: 8 -> 4, of which waited for: 6 -> 4; matrix products, arithmetic and copies ran while one was open for 2% -> 1% of each run, Pallas kernels for 2% -> 2%
where the time goes in v2:
time: 110 us
  blocking collectives  36.1 us (33%)
  waiting for transfers between devices  22.3 us (20%)
  starting transfers between devices  19.8 us (18%)
  Pallas kernels  19 us (17%)
  local copies, waits for them, and re-layouts  11.5 us (10%)
    all_to_all x1, blocking collectives, shards(): got = lax.all_to_all(half, 'panel', 0, 0, axis_index_groups=same_core)  21.9 us
    all_to_all x2, waiting for transfers between devices, spread(): lax.all_to_all(jnp.broadcast_to(values[None], (count, *values.shape)), ax...  19.5 us
    all_to_all x2, starting transfers between devices, spread(): lax.all_to_all(jnp.broadcast_to(values[None], (count, *values.shape)), ax...  16.9 us
    pallas_call x1, Pallas kernels, local(): pl.pallas_call(edges, out_shape=outs, in_specs=[pl.BlockSpec(memory_space...  16.7 us
    all_to_all x1, blocking collectives, spread(): lax.all_to_all(jnp.broadcast_to(values[None], (count, *values.shape)), ax...  14.1 us
    unnamed x29, local copies, waits for them, and re-layouts  6.26 us
    broadcast_in_dim x3, local copies, waits for them, and re-layouts, spread(): jnp.broadcast_to(values[None], (count, *values.shape))  2.51 us
    ppermute x1, starting transfers between devices, shards(): x_other = lax.ppermute(x_own, 'panel', siblings)  2.49 us
  transfers between devices with their start and end apart: 4, of which 4 were waited for; matrix products, arithmetic and copies ran while one was open for 1% of the time, Pallas kernels for 2%

profile of v2, /device:TPU:1, one launch (start us, length us, event | category | flops | bytes accessed | tf_op | source)
XLA Modules:
  0.0 109.7 jit_solution(16664651319256373359)
XLA Ops:
  0.7 1.8 %broadcast_in_dim.6 = bf16[16,128,128]{2,1,0:T(8,128)(2,1)} broadcast(bf16[128,128]{1,0:T(8,128)(2,1)} %param.10), dimensions={1,2} | broadcast | bytes 557056 | tf_op jit(solution)/shard_map/broadcast_in_dim | solution.py:360
  2.4 10.1 %all-to-all-start = ((bf16[16,128,128]{2,1,0:T(8,128)(2,1)}), bf16[16,128,128]{2,1,0:T(8,128)(2,1)S(1)}, u32[]{:S(2)}, u32[]{:S(2)}) async-start(bf16[16,128,128]{2,1,0:T(8,128)(2,1)} %broadcast_in_dim.6), calls=%async_computation | async-start | bytes 1048576 | tf_op jit(solution)/shard_map/all_to_all | solution.py:359
  12.8 0.9 copy-done.2
  13.7 0.9 copy-done.4
  14.6 2.2 %prepare.1 = (bf16[512,512]{1,0:T(8,128)(2,1)S(1)}, bf16[512,512]{1,0:T(8,128)(2,1)S(1)}, f32[16,128,128]{2,1,0:T(8,128)S(1)}, f32[4,8,128]{2,1,0:T(8,128)S(1)},...) custom-call(bf16[512,128]{1,0:T(8,128)(2,1)S(1)} %copy-done.2, bf16[128,512]{1,0:T(8,128)(2,1)S(1)} %copy-done.4, ...), custom_call_target="tpu_custom_call" | custom-call | flops 67108864 | bytes 6291456 | tf_op jit(solution)/shard_map/prepare/pallas_call | solution.py:285
  16.8 0.8 copy-done.6
  17.6 0.8 copy-done.8
  18.5 9.7 %all-to-all-done = bf16[16,128,128]{2,1,0:T(8,128)(2,1)S(1)} async-done(((bf16[16,128,128]{2,1,0:T(8,128)(2,1)}), bf16[16,128,128]{2,1,0:T(8,128)(2,1)S(1)}, u32[]{:S(2)}, u32[]{:S(2)}) %all-to-all-start) | async-done | bytes 524320 | tf_op jit(solution)/shard_map/all_to_all | solution.py:359
  28.2 2.5 %collective-permute-start = (bf16[2048,128]{1,0:T(8,128)(2,1)S(1)}, bf16[2048,128]{1,0:T(8,128)(2,1)S(1)}, u32[]{:S(2)}, u32[]{:S(2)}) collective-permute-start(bf16[2048,128]{1,0:T(8,128)(2,1)S(1)} %bitcast.8), channel_id=1, source_target_pairs={{0,8},{8,0},{16,24},{24,16},{32,40},{40,32},{48,56},{56,48},{64,72... | collective-permute-start | bytes 1572872 | tf_op jit(solution)/shard_map/ppermute | solution.py:367
  31.1 1.1 %collective-permute-done.x_other_ref = bf16[2048,128]{1,0:T(8,128)(2,1)S(1)} collective-permute-done((bf16[2048,128]{1,0:T(8,128)(2,1)S(1)}, bf16[2048,128]{1,0:T(8,128)(2,1)S(1)}, u32[]{:S(2)}, u32[]{:S(2)}) %collective-permute-start) | collective-permute-done | bytes 524320 | tf_op jit(solution)/shard_map/ppermute | solution.py:367
  32.3 1.0 copy-done.7
  33.3 1.0 copy-done.9
  34.3 16.7 %edges.1 = (f32[512,128]{1,0:T(8,128)}, f32[16,152,128]{2,1,0:T(8,128)S(1)}, bf16[16,152,128]{2,1,0:T(8,128)(2,1)S(1)}) custom-call(s32[16]{0:T(128)S(1)} %copy-done.10, s32[16]{0:T(128)S(1)} %copy-done.11, s32[1]{0:T(128)} %bitcast.place_ref, bf16[2048,128]{1,0:T(8,128)(2,1)S(1)} %bitcast.9, bf16[2048,128]{1,0:T(8,128)(2,1)S(1)} %collective-permute-done.x_other_ref, ...), custom_call_target="tpu_custom_call" | custom-call | flops 4294967296 | bytes 12582912 | tf_op jit(solution)/shard_map/edges/pallas_call | solution.py:323
  51.1 0.4 collective-permute-start.1
  51.4 1.7 %collective-permute-done.1 = bf16[16,152,128]{2,1,0:T(8,128)(2,1)S(1)} collective-permute-done((bf16[16,152,128]{2,1,0:T(8,128)(2,1)S(1)}, bf16[16,152,128]{2,1,0:T(8,128)(2,1)S(1)}, u32[]{:S(2)}, u32[]{:S(2)}) %collective-permute-start.1) | collective-permute-done | bytes 622624 | tf_op jit(solution)/shard_map/ppermute | solution.py:372
  53.3 21.9 %all_to_all.20 = bf16[16,152,128]{2,1,0:T(8,128)(2,1)S(1)} all-to-all(bf16[16,152,128]{2,1,0:T(8,128)(2,1)S(1)} %add_convert_fusion), channel_id=1, replica_groups={{0,16,32,48,64,80,96,112,128,144,160,176,192,208,224,240},{8,24,40,56,7..., dimensions={0} | all-to-all | bytes 1245184 | tf_op jit(solution)/shard_map/all_to_all | solution.py:373
  75.3 14.1 %all_to_all.21 = bf16[8,152,128]{2,1,0:T(8,128)(2,1)S(1)} all-to-all(bf16[8,152,128]{2,1,0:T(8,128)(2,1)S(1)} %broadcast_in_dim.7), channel_id=1, replica_groups=mesh['panel'=32,'rep'=8] {'rep'}, dimensions={0} | all-to-all | bytes 622592 | tf_op jit(solution)/shard_map/all_to_all | solution.py:359
  89.5 0.7 broadcast_in_dim.8
  90.2 6.8 %all-to-all-start.3 = ((bf16[32,24,128]{2,1,0:T(8,128)(2,1)}), bf16[32,24,128]{2,1,0:T(8,128)(2,1)S(1)}, u32[]{:S(2)}, u32[]{:S(2)}) async-start(bf16[32,24,128]{2,1,0:T(8,128)(2,1)} %broadcast_in_dim.8), calls=%async_computation.3 | async-start | bytes 393216 | tf_op jit(solution)/shard_map/all_to_all | solution.py:359
  97.0 0.6 slice.26
  97.7 9.7 %all-to-all-done.3 = bf16[32,24,128]{2,1,0:T(8,128)(2,1)S(1)} async-done(((bf16[32,24,128]{2,1,0:T(8,128)(2,1)}), bf16[32,24,128]{2,1,0:T(8,128)(2,1)S(1)}, u32[]{:S(2)}, u32[]{:S(2)}) %all-to-all-start.3) | async-done | bytes 196640 | tf_op jit(solution)/shard_map/all_to_all | solution.py:359
  107.4 0.7 squeeze.7
  108.1 0.7 squeeze.6
  108.9 0.7 copy.23
  (34 shorter events, 1.1 us)
Async XLA Ops:
  0.6 11.9 %copy-start.12 = (f32[8,64]{1,0:T(8,128)S(1)}, f32[8,64]{1,0:T(8,128)}, u32[]{:S(2)}) copy-start(f32[8,64]{1,0:T(8,128)} %param.13) | copy-start | bytes 6148
  0.6 12.1 %copy-start.13 = (f32[8,64]{1,0:T(8,128)S(1)}, f32[8,64]{1,0:T(8,128)}, u32[]{:S(2)}) copy-start(f32[8,64]{1,0:T(8,128)} %param.14) | copy-start | bytes 6148
  0.7 12.1 %copy-start = (s32[16,128,128]{2,1,0:T(8,128)S(1)}, s32[16,128,128]{2,1,0:T(8,128)}, u32[]{:S(2)}) copy-start(s32[16,128,128]{2,1,0:T(8,128)} %mask_ref.1) | copy-start | bytes 3145732
  0.7 12.1 %copy-start.1 = (bf16[512,512]{1,0:T(8,128)(2,1)S(1)}, bf16[512,512]{1,0:T(8,128)(2,1)}, u32[]{:S(2)}) copy-start(bf16[512,512]{1,0:T(8,128)(2,1)} %grad_ref.1) | copy-start | bytes 1572868
  2.4 25.8 %all-to-all-start = ((bf16[16,128,128]{2,1,0:T(8,128)(2,1)}), bf16[16,128,128]{2,1,0:T(8,128)(2,1)S(1)}, u32[]{:S(2)}, u32[]{:S(2)}) async-start(bf16[16,128,128]{2,1,0:T(8,128)(2,1)} %broadcast_in_dim.6), calls=%async_computation | async-start | bytes 1048576 | tf_op jit(solution)/shard_map/all_to_all | solution.py:359
  12.6 19.6 %copy-start.10 = (s32[16]{0:T(128)S(1)}, s32[16]{0:T(128)}, u32[]{:S(2)}) copy-start(s32[16]{0:T(128)} %rows_ref.1) | copy-start | bytes 196
  12.6 19.6 %copy-start.11 = (s32[16]{0:T(128)S(1)}, s32[16]{0:T(128)}, u32[]{:S(2)}) copy-start(s32[16]{0:T(128)} %cols_ref.1) | copy-start | bytes 196
  12.8 0.9 copy-start.2
  13.7 0.9 copy-start.4
  14.6 17.6 %copy-start.3 = (bf16[512,128]{1,0:T(8,128)(2,1)S(1)}, bf16[512,128]{1,0:T(8,128)(2,1)}, u32[]{:S(2)}) copy-start(bf16[512,128]{1,0:T(8,128)(2,1)} %x_dst_ref.3) | copy-start | bytes 393220
  14.6 17.7 %copy-start.5 = (bf16[128,512]{1,0:T(8,128)(2,1)S(1)}, bf16[128,512]{1,0:T(8,128)(2,1)}, u32[]{:S(2)}) copy-start(bf16[128,512]{1,0:T(8,128)(2,1)} %weight_ref.3) | copy-start | bytes 393220
  16.8 0.8 copy-start.6
  17.6 0.8 copy-start.8
  28.2 4.0 %collective-permute-start = (bf16[2048,128]{1,0:T(8,128)(2,1)S(1)}, bf16[2048,128]{1,0:T(8,128)(2,1)S(1)}, u32[]{:S(2)}, u32[]{:S(2)}) collective-permute-start(bf16[2048,128]{1,0:T(8,128)(2,1)S(1)} %bitcast.8), channel_id=1, source_target_pairs={{0,8},{8,0},{16,24},{24,16},{32,40},{40,32},{48,56},{56,48},{64,72... | collective-permute-start | bytes 1572872 | tf_op jit(solution)/shard_map/ppermute | solution.py:367
  32.2 1.0 copy-start.7
  33.3 1.0 copy-start.9
  51.1 2.1 %collective-permute-start.1 = (bf16[16,152,128]{2,1,0:T(8,128)(2,1)S(1)}, bf16[16,152,128]{2,1,0:T(8,128)(2,1)S(1)}, u32[]{:S(2)}, u32[]{:S(2)}) collective-permute-start(bf16[16,152,128]{2,1,0:T(8,128)(2,1)S(1)} %get-tuple-element.27), channel_id=1, source_target_pairs={{0,8},{8,0},{16,24},{24,16},{32,40},{40,32},{48,56},{56,48},{64,72... | collective-permute-start | bytes 1867784 | tf_op jit(solution)/shard_map/ppermute | solution.py:372
  90.2 17.2 %all-to-all-start.3 = ((bf16[32,24,128]{2,1,0:T(8,128)(2,1)}), bf16[32,24,128]{2,1,0:T(8,128)(2,1)S(1)}, u32[]{:S(2)}, u32[]{:S(2)}) async-start(bf16[32,24,128]{2,1,0:T(8,128)(2,1)} %broadcast_in_dim.8), calls=%async_computation.3 | async-start | bytes 393216 | tf_op jit(solution)/shard_map/all_to_all | solution.py:359

commit v3 on v2

--- a/solution.py
+++ b/solution.py
@@ -32,10 +32,15 @@
     return hi, mid, (rest - mid.astype(F32)).astype(BF16)
 
 
-def head_rows(att_flat):
+def head_rows(att):
     head = lax.broadcasted_iota(jnp.int32, (HEADS, WIDTH), 0)
     lane = lax.broadcasted_iota(jnp.int32, (HEADS, WIDTH), 1) // HEAD_DIM
-    return jnp.where(head == lane, jnp.broadcast_to(att_flat, (HEADS, WIDTH)), 0.0)
+    return jnp.where(head == lane, jnp.concatenate([att] * HEADS, axis=1), 0.0)
+
+
+def feature_rows(att):
+    flat = jnp.sum(head_rows(att), axis=0, keepdims=True)
+    return jnp.broadcast_to(flat, (LANES, WIDTH)).T
 
 
 def per_head(rows):
@@ -89,7 +94,7 @@
 
 def edges(
     rows_ref, cols_ref, place_ref,
-    x_own_ref, x_other_ref, x_dst_ref, weight_ref, att_src_ref, att_src_col_ref, att_dst_col_ref,
+    x_own_ref, x_other_ref, x_dst_ref, weight_ref, att_src_ref, att_dst_ref,
     proj_ref, grad_t_ref, mask_t_ref, score_ref, self_ref, slope_ref, pair_ref,
     grad_dst_ref, keep_ref, send_ref,
     proj_src, tiles, acc, scaled, scaled_c, own, grad_src_ref, grad_weight_ref, rows_out, score_cols, att_wide, x_all,
@@ -104,7 +109,7 @@
     grad_src_ref[...] = jnp.zeros(grad_src_ref.shape, grad_src_ref.dtype)
     ones = jnp.ones((ext - HEAD_DIM, BLK), BF16)
 
-    att_wide[...] = jnp.broadcast_to(att_src_col_ref[...], att_wide.shape)
+    att_wide[...] = feature_rows(att_src_ref[...])
 
     core = place_ref[0] % 2
     half = x_own_ref.shape[0]
@@ -188,7 +193,7 @@
             ).astype(BF16)
 
     att_src_wide = att_wide[...]
-    att_dst_wide = jnp.broadcast_to(att_dst_col_ref[...], att_wide.shape)
+    att_dst_wide = feature_rows(att_dst_ref[...])
     grad_weight = jnp.zeros((WIDTH, IN), F32)
     att_sums = jnp.zeros((WIDTH, 32), F32)
     for r in range(dest_blocks):
@@ -244,12 +249,13 @@
     pick = head == feat
     src = jnp.where(pick, sums[:, 0:8] + sums[:, 8:16], 0.0)
     dst = jnp.where(pick, sums[:, 16:24] + sums[:, 24:32], 0.0)
-    att_rows8 = [
-        jnp.sum(part[f : f + LANES].T, axis=0, keepdims=True)
-        for part in (src, dst)
-        for f in range(0, WIDTH, LANES)
-    ]
-    att8 = jnp.concatenate(att_rows8, axis=0)
+    low = lax.broadcasted_iota(jnp.int32, (HEADS, LANES), 1) < HEAD_DIM
+    folded = []
+    for part in (src, dst):
+        part = part.T
+        pair = sum(part[:, f : f + LANES] for f in range(0, WIDTH, LANES))
+        folded.append(pair + pltpu.roll(pair, HEAD_DIM, axis=1))
+    att8 = jnp.where(low, folded[0], folded[1])
     for f in range(0, WIDTH, LANES):
         rows_out[f : f + LANES, :] = grad_weight_ref[f : f + LANES, :].T
 
@@ -279,7 +285,6 @@
     slots = block_masks.shape[0]
     dest = x_dst.shape[0]
     dest_blocks = dest // BLK
-    att_src_row, att_dst_row = att_src.reshape(1, WIDTH), att_dst.reshape(1, WIDTH)
     params = pltpu.CompilerParams(vmem_limit_bytes=VMEM_BYTES)
     rows8 = jax.ShapeDtypeStruct((HEADS, dest), F32)
     return pl.pallas_call(
@@ -294,7 +299,7 @@
         compiler_params=params,
         cost_estimate=pl.CostEstimate(flops=2 * dest * IN * WIDTH, bytes_accessed=6 << 20, transcendentals=0),
         name="prepare",
-    )(x_dst, weight, att_src_row, att_dst_row, grad_out, block_masks)
+    )(x_dst, weight, att_src, att_dst, grad_out, block_masks)
 
 
 def local(x_own, x_other, x_dst, weight, att_src, att_dst, block_rows, block_cols, place, prepared):
@@ -304,12 +309,10 @@
     dest_blocks = dest // BLK
     sources = 2 * x_own.shape[0]
     panels = sources // BLK
-    att_src_row = att_src.reshape(1, WIDTH)
-    att_src_col, att_dst_col = att_src.reshape(WIDTH, 1), att_dst.reshape(WIDTH, 1)
     params = pltpu.CompilerParams(vmem_limit_bytes=VMEM_BYTES)
     ext = 80
     operands = (
-        x_own, x_other, x_dst, weight, att_src_row, att_src_col, att_dst_col,
+        x_own, x_other, x_dst, weight, att_src, att_dst,
         proj, grad_t, mask_t, score, self_w, slope, pair,
     )
     units = panels // 2
@@ -362,8 +365,6 @@
 
     x_own = spread(x_src, "panel", units, same_core).reshape(-1, IN)
     prepared = prep(x_dst, weight, att_src, att_dst, grad_out, block_masks)
-    x_own, slope = lax.optimization_barrier((x_own, prepared[5]))
-    prepared = [*prepared[:5], slope, *prepared[6:]]
     x_other = lax.ppermute(x_own, "panel", siblings)
     place = lax.axis_index("panel").reshape(1)
     grad_dst, keep, send = local(
@@ -374,10 +375,10 @@
     unit = got.astype(F32).sum(axis=0).astype(BF16)
     total = spread(unit, "rep", lax.axis_size("rep")).astype(F32).sum(axis=0)
     grad_src = total[:BLK]
-    small = spread(total[BLK:].astype(BF16), "panel", panels).astype(F32)
+    small = spread(total[BLK:].astype(BF16), "panel", panels)
     grad_weight = small[:, :share].reshape(WIDTH // LANES, IN, LANES).transpose(1, 0, 2).reshape(IN, WIDTH)
-    att = small[0, share:].reshape(2, HEADS, HEAD_DIM)
-    return grad_src, grad_dst, grad_weight, att[0], att[1]
+    att = small[0, share:].astype(F32)
+    return grad_src, grad_dst, grad_weight.astype(F32), att[:, :HEAD_DIM], att[:, HEAD_DIM:]
 
 
 def solution(mesh):

time: 110 us -> 109 us (level)
  blocking collectives: 36.1 us -> 61.8 us
  starting transfers between devices: 19.8 us -> 9.18 us
  waiting for transfers between devices: 22.3 us -> 11.8 us
  local copies, waits for them, and re-layouts: 11.5 us -> 4.86 us
    all_to_all x1 -> x2, blocking collectives: 14.1 us -> 39.7 us  [spread(): lax.all_to_all(jnp.broadcast_to(values[None], (count, *values.shape)), ax...]
    all_to_all x2 -> x1, starting transfers between devices: 16.9 us -> 6.66 us  [spread(): lax.all_to_all(jnp.broadcast_to(values[None], (count, *values.shape)), ax...]
    all_to_all x2 -> x1, waiting for transfers between devices: 19.5 us -> 9.73 us  [spread(): lax.all_to_all(jnp.broadcast_to(values[None], (count, *values.shape)), ax...]
    unnamed x29 -> x16, local copies, waits for them, and re-layouts: 6.26 us -> 1.83 us
    squeeze x2 -> x0, local copies, waits for them, and re-layouts: 1.34 us -> none  [shards(): return (grad_src, grad_dst, grad_weight, att[0], att[1])]
    ppermute x1, waiting for transfers between devices: 1.12 us -> 0.01 us  [shards(): x_other = lax.ppermute(x_own, 'panel', siblings)]
  transfers between devices with their start and end apart: 4 -> 3, of which waited for: 4 -> 2; matrix products, arithmetic and copies ran while one was open for 1% -> 1% of each run, Pallas kernels for 2% -> 2%
where the time goes in v3:
time: 109 us; the launch traced here: 108 us
  blocking collectives  61.8 us (57%)
  Pallas kernels  19 us (17%)
  waiting for transfers between devices  11.8 us (11%)
  starting transfers between devices  9.18 us (8%)
  local copies, waits for them, and re-layouts  4.86 us (4%)
    all_to_all x2, blocking collectives, spread(): lax.all_to_all(jnp.broadcast_to(values[None], (count, *values.shape)), ax...  39.7 us
    all_to_all x1, blocking collectives, shards(): got = lax.all_to_all(half, 'panel', 0, 0, axis_index_groups=same_core)  22.1 us
    pallas_call x1, Pallas kernels, local(): pl.pallas_call(edges, out_shape=outs, in_specs=[pl.BlockSpec(memory_space...  16.8 us
    all_to_all x1, waiting for transfers between devices, spread(): lax.all_to_all(jnp.broadcast_to(values[None], (count, *values.shape)), ax...  9.73 us
    all_to_all x1, starting transfers between devices, spread(): lax.all_to_all(jnp.broadcast_to(values[None], (count, *values.shape)), ax...  6.66 us
    ppermute x1, starting transfers between devices, shards(): x_other = lax.ppermute(x_own, 'panel', siblings)  2.49 us
    pallas_call x1, Pallas kernels, prep(): pl.pallas_call(prepare, out_shape=[jax.ShapeDtypeStruct((WIDTH, dest), BF...  2.22 us
  transfers between devices with their start and end apart: 3, of which 2 were waited for; matrix products, arithmetic and copies ran while one was open for 1% of the time, Pallas kernels for 2%

profile of v3, /device:TPU:1, one launch (start us, length us, event | category | flops | bytes accessed | tf_op | source)
XLA Modules:
  0.0 108.4 jit_solution(14025490413560843907)
XLA Ops:
  0.6 0.0 copy-start.5
  0.7 1.0 broadcast_in_dim.6
  1.6 0.0 copy-start.6
  1.7 0.0 copy-start.7
  1.7 25.6 %all_to_all.20 = bf16[16,128,128]{2,1,0:T(8,128)(2,1)S(1)} all-to-all(bf16[16,128,128]{2,1,0:T(8,128)(2,1)S(1)} %broadcast_in_dim.6), channel_id=1, replica_groups={{0,16,32,48,64,80,96,112,128,144,160,176,192,208,224,240},{8,24,40,56,7..., dimensions={0} | all-to-all | bytes 1048576 | tf_op jit(solution)/shard_map/all_to_all | solution.py:362
  27.2 2.5 %collective-permute-start = (bf16[2048,128]{1,0:T(8,128)(2,1)S(1)}, bf16[2048,128]{1,0:T(8,128)(2,1)S(1)}, u32[]{:S(2)}, u32[]{:S(2)}) collective-permute-start(bf16[2048,128]{1,0:T(8,128)(2,1)S(1)} %bitcast.19), channel_id=1, source_target_pairs={{0,8},{8,0},{16,24},{24,16},{32,40},{40,32},{48,56},{56,48},{64,72... | collective-permute-start | bytes 1572872 | tf_op jit(solution)/shard_map/ppermute | solution.py:368
  29.7 0.0 copy-start.2
  29.7 0.9 copy-done.2
  30.6 0.9 copy-done.3
  31.5 2.2 %prepare.1 = (bf16[512,512]{1,0:T(8,128)(2,1)S(1)}, bf16[512,512]{1,0:T(8,128)(2,1)S(1)}, f32[16,128,128]{2,1,0:T(8,128)S(1)}, f32[4,8,128]{2,1,0:T(8,128)S(1)},...) custom-call(bf16[512,128]{1,0:T(8,128)(2,1)S(1)} %copy-done.2, bf16[128,512]{1,0:T(8,128)(2,1)S(1)} %copy-done.3, ...), custom_call_target="tpu_custom_call" | custom-call | flops 67108864 | bytes 6291456 | tf_op jit(solution)/shard_map/prepare/pallas_call | solution.py:290
  33.8 0.0 collective-permute-done.x_other_ref
  33.8 16.8 %edges.1 = (f32[512,128]{1,0:T(8,128)}, f32[16,152,128]{2,1,0:T(8,128)S(1)}, bf16[16,152,128]{2,1,0:T(8,128)(2,1)S(1)}) custom-call(s32[16]{0:T(128)S(1)} %copy-done.6, s32[16]{0:T(128)S(1)} %copy-done.7, s32[1]{0:T(128)} %bitcast.place_ref, bf16[2048,128]{1,0:T(8,128)(2,1)S(1)} %bitcast.20, bf16[2048,128]{1,0:T(8,128)(2,1)S(1)} %collective-permute-done.x_other_ref, ...), custom_call_target="tpu_custom_call" | custom-call | flops 4294967296 | bytes 12582912 | tf_op jit(solution)/shard_map/edges/pallas_call | solution.py:326
  50.6 0.0 collective-permute-start.1
  50.7 2.0 %collective-permute-done.1 = bf16[16,152,128]{2,1,0:T(8,128)(2,1)S(1)} collective-permute-done((bf16[16,152,128]{2,1,0:T(8,128)(2,1)S(1)}, bf16[16,152,128]{2,1,0:T(8,128)(2,1)S(1)}, u32[]{:S(2)}, u32[]{:S(2)}) %collective-permute-start.1) | collective-permute-done | bytes 622624 | tf_op jit(solution)/shard_map/ppermute | solution.py:373
  52.7 0.1 add_convert_fusion
  52.8 22.1 %all_to_all.21 = bf16[16,152,128]{2,1,0:T(8,128)(2,1)S(1)} all-to-all(bf16[16,152,128]{2,1,0:T(8,128)(2,1)S(1)} %add_convert_fusion), channel_id=1, replica_groups={{0,16,32,48,64,80,96,112,128,144,160,176,192,208,224,240},{8,24,40,56,7..., dimensions={0} | all-to-all | bytes 1245184 | tf_op jit(solution)/shard_map/all_to_all | solution.py:374
  74.9 0.1 reduce_sum.21
  75.0 14.2 %all_to_all.22 = bf16[8,152,128]{2,1,0:T(8,128)(2,1)S(1)} all-to-all(bf16[8,152,128]{2,1,0:T(8,128)(2,1)S(1)} %broadcast_in_dim.7), channel_id=1, replica_groups=mesh['panel'=32,'rep'=8] {'rep'}, dimensions={0} | all-to-all | bytes 622592 | tf_op jit(solution)/shard_map/all_to_all | solution.py:362
  89.2 0.7 broadcast_in_dim.8
  89.9 6.7 %all-to-all-start.3 = ((bf16[32,24,128]{2,1,0:T(8,128)(2,1)}), bf16[32,24,128]{2,1,0:T(8,128)(2,1)S(1)}, u32[]{:S(2)}, u32[]{:S(2)}) async-start(bf16[32,24,128]{2,1,0:T(8,128)(2,1)} %broadcast_in_dim.8), calls=%async_computation.3 | async-start | bytes 393216 | tf_op jit(solution)/shard_map/all_to_all | solution.py:362
  96.6 0.6 slice.25
  97.3 9.7 %all-to-all-done.3 = bf16[32,24,128]{2,1,0:T(8,128)(2,1)S(1)} async-done(((bf16[32,24,128]{2,1,0:T(8,128)(2,1)}), bf16[32,24,128]{2,1,0:T(8,128)(2,1)S(1)}, u32[]{:S(2)}, u32[]{:S(2)}) %all-to-all-start.3) | async-done | bytes 196640 | tf_op jit(solution)/shard_map/all_to_all | solution.py:362
  107.0 0.7 fusion.1
  107.7 0.7 copy_bitcast_fusion
  (15 shorter events, 0.1 us)
Async XLA Ops:
  0.6 29.1 %copy-start.5 = (f32[8,64]{1,0:T(8,128)S(1)}, f32[8,64]{1,0:T(8,128)}, u32[]{:S(2)}) copy-start(f32[8,64]{1,0:T(8,128)} %att_dst_ref.3) | copy-start | bytes 6148
  0.6 29.1 %copy-start.4 = (f32[8,64]{1,0:T(8,128)S(1)}, f32[8,64]{1,0:T(8,128)}, u32[]{:S(2)}) copy-start(f32[8,64]{1,0:T(8,128)} %att_src_ref.3) | copy-start | bytes 6148
  0.7 29.1 %copy-start = (s32[16,128,128]{2,1,0:T(8,128)S(1)}, s32[16,128,128]{2,1,0:T(8,128)}, u32[]{:S(2)}) copy-start(s32[16,128,128]{2,1,0:T(8,128)} %mask_ref.1) | copy-start | bytes 3145732
  0.7 29.1 %copy-start.1 = (bf16[512,512]{1,0:T(8,128)(2,1)S(1)}, bf16[512,512]{1,0:T(8,128)(2,1)}, u32[]{:S(2)}) copy-start(bf16[512,512]{1,0:T(8,128)(2,1)} %grad_ref.1) | copy-start | bytes 1572868
  1.6 32.1 %copy-start.6 = (s32[16]{0:T(128)S(1)}, s32[16]{0:T(128)}, u32[]{:S(2)}) copy-start(s32[16]{0:T(128)} %rows_ref.1) | copy-start | bytes 196
  1.7 32.1 %copy-start.7 = (s32[16]{0:T(128)S(1)}, s32[16]{0:T(128)}, u32[]{:S(2)}) copy-start(s32[16]{0:T(128)} %cols_ref.1) | copy-start | bytes 196
  27.2 6.5 %collective-permute-start = (bf16[2048,128]{1,0:T(8,128)(2,1)S(1)}, bf16[2048,128]{1,0:T(8,128)(2,1)S(1)}, u32[]{:S(2)}, u32[]{:S(2)}) collective-permute-start(bf16[2048,128]{1,0:T(8,128)(2,1)S(1)} %bitcast.19), channel_id=1, source_target_pairs={{0,8},{8,0},{16,24},{24,16},{32,40},{40,32},{48,56},{56,48},{64,72... | collective-permute-start | bytes 1572872 | tf_op jit(solution)/shard_map/ppermute | solution.py:368
  29.7 0.9 copy-start.2
  30.6 0.9 copy-start.3
  50.6 2.1 %collective-permute-start.1 = (bf16[16,152,128]{2,1,0:T(8,128)(2,1)S(1)}, bf16[16,152,128]{2,1,0:T(8,128)(2,1)S(1)}, u32[]{:S(2)}, u32[]{:S(2)}) collective-permute-start(bf16[16,152,128]{2,1,0:T(8,128)(2,1)S(1)} %get-tuple-element.23), channel_id=1, source_target_pairs={{0,8},{8,0},{16,24},{24,16},{32,40},{40,32},{48,56},{56,48},{64,72... | collective-permute-start | bytes 1867784 | tf_op jit(solution)/shard_map/ppermute | solution.py:373
  89.9 17.0 %all-to-all-start.3 = ((bf16[32,24,128]{2,1,0:T(8,128)(2,1)}), bf16[32,24,128]{2,1,0:T(8,128)(2,1)S(1)}, u32[]{:S(2)}, u32[]{:S(2)}) async-start(bf16[32,24,128]{2,1,0:T(8,128)(2,1)} %broadcast_in_dim.8), calls=%async_computation.3 | async-start | bytes 393216 | tf_op jit(solution)/shard_map/all_to_all | solution.py:362

commit v4 on v3

--- a/solution.py
+++ b/solution.py
@@ -66,15 +66,30 @@
 
 
 def prepare(
-    x_dst_ref, weight_ref, att_src_ref, att_dst_ref, grad_ref, mask_ref,
+    x_dst_hbm, weight_hbm, att_src_ref, att_dst_ref, grad_ref, mask_ref,
     proj_ref, grad_t_ref, mask_t_ref, score_ref, self_ref, slope_ref, pair_ref,
+    x_dst_ref, weight_ref, x_sem, weight_sem,
 ):
+    copies = (
+        pltpu.make_async_copy(x_dst_hbm, x_dst_ref, x_sem),
+        pltpu.make_async_copy(weight_hbm, weight_ref, weight_sem),
+    )
+    for copy in copies:
+        copy.start()
+
+    def turn(b, carry):
+        mask_t_ref[b] = mask_ref[b].astype(F32).T
+        return carry
+
+    lax.fori_loop(0, mask_ref.shape[0], turn, 0, unroll=4)
+    grad_t = grad_ref[...].astype(F32).T
+    grad_t_ref[...] = grad_t.astype(BF16)
+    parts = split3(head_rows(att_dst_ref[...])) + split3(head_rows(att_src_ref[...]))
+    for copy in copies:
+        copy.wait()
     weight_t = weight_ref[...].astype(F32).T.astype(BF16)
     proj = mm(weight_t, x_dst_ref[...], NT).astype(BF16)
     proj_ref[...] = proj
-    grad_t = grad_ref[...].astype(F32).T
-    grad_t_ref[...] = grad_t.astype(BF16)
-    parts = split3(head_rows(att_dst_ref[...])) + split3(head_rows(att_src_ref[...]))
     scores = mm(jnp.concatenate(parts, axis=0), proj)
     score_d = (scores[0:8] + scores[8:16]) + scores[16:24]
     score_own = (scores[24:32] + scores[32:40]) + scores[40:48]
@@ -85,28 +100,27 @@
     slope_ref[...] = slope_self
     pair_ref[...] = head_sums(grad_t * proj.astype(F32))
 
-    def turn(b, carry):
-        mask_t_ref[b] = mask_ref[b].astype(F32).T
-        return carry
-
-    lax.fori_loop(0, mask_ref.shape[0], turn, 0)
-
 
 def edges(
     rows_ref, cols_ref, place_ref,
-    x_own_ref, x_other_ref, x_dst_ref, weight_ref, att_src_ref, att_dst_ref,
+    x_own_ref, x_other_ref, x_dst_hbm, weight_hbm, att_src_ref, att_dst_ref,
     proj_ref, grad_t_ref, mask_t_ref, score_ref, self_ref, slope_ref, pair_ref,
     grad_dst_ref, keep_ref, send_ref,
-    proj_src, tiles, acc, scaled, scaled_c, own, grad_src_ref, grad_weight_ref, rows_out, score_cols, att_wide, x_all,
+    proj_src, tiles, acc, scaled, scaled_c, own, grad_src_ref, grad_weight_ref, rows_out, score_cols, att_wide, x_all, x_dst_ref, weight_ref, x_sem, weight_sem,
 ):
     slots = mask_t_ref.shape[0]
     dest_blocks = acc.shape[0]
     ext = acc.shape[2]
+    weight_copy = pltpu.make_async_copy(weight_hbm, weight_ref, weight_sem)
+    x_dst_copy = pltpu.make_async_copy(x_dst_hbm, x_dst_ref, x_sem)
+    weight_copy.start()
+    x_dst_copy.start()
+    acc[...] = jnp.zeros(acc.shape, F32)
+    grad_src_ref[...] = jnp.zeros(grad_src_ref.shape, grad_src_ref.dtype)
+    att_rows = jnp.concatenate(split3(head_rows(att_src_ref[...])), axis=0)
+    weight_copy.wait()
     weight = weight_ref[...]
     weight_t = weight.astype(F32).T.astype(BF16)
-    att_rows = jnp.concatenate(split3(head_rows(att_src_ref[...])), axis=0)
-    acc[...] = jnp.zeros(acc.shape, F32)
-    grad_src_ref[...] = jnp.zeros(grad_src_ref.shape, grad_src_ref.dtype)
     ones = jnp.ones((ext - HEAD_DIM, BLK), BF16)
 
     att_wide[...] = feature_rows(att_src_ref[...])
@@ -142,16 +156,17 @@
             pre2 = jnp.broadcast_to(cols[:, h : h + 1], (BLK, BLK)) + score_d[h : h + 1]
             weight_e, slope = weight_and_slope(pre2)
             weight_e = weight_e * mask
-            pair = jnp.concatenate(
-                [weight_e.astype(BF16), (weight_e * slope).astype(BF16)], axis=1
-            )
-            tiles[b, h] = pair
+            both = [weight_e.astype(BF16), (weight_e * slope).astype(BF16)]
+            tiles[b, h, 0:BLK] = both[0]
+            tiles[b, h, BLK : 2 * BLK] = both[1]
+            pair = jnp.concatenate(both, axis=1)
             left = jnp.concatenate([proj[h * HEAD_DIM : (h + 1) * HEAD_DIM], ones], axis=0)
             acc[row, h] += mm(left, pair)
         return carry
 
-    lax.fori_loop(0, slots, forward, 0, unroll=4)
-
+    lax.fori_loop(0, slots, forward, 0, unroll=8)
+
+    x_dst_copy.wait()
     self_att_rows, self_grad_rows, grad_d_rows = [], [], []
     for r in range(dest_blocks):
         lanes = slice(r * BLK, (r + 1) * BLK)
@@ -215,9 +230,7 @@
         proj = proj_src[b]
         feats, grads = [], []
         for h in range(HEADS):
-            pair = tiles[b, h]
-            stack = jnp.concatenate([pair[:, :BLK], pair[:, BLK:]], axis=0)
-            out = mm(scaled[row, h], stack, NT)
+            out = mm(scaled[row, h], tiles[b, h], NT)
             feats.append(out[:HEAD_DIM, :BLK])
             proj_h = proj[h * HEAD_DIM : (h + 1) * HEAD_DIM].astype(F32)
             grads.append(
@@ -296,6 +309,14 @@
             jax.ShapeDtypeStruct((dest_blocks, HEADS, BLK), F32),
             rows8, rows8, rows8,
         ],
+        in_specs=[pl.BlockSpec(memory_space=pltpu.HBM)] * 2 + [pl.BlockSpec(memory_space=pltpu.VMEM)] * 4,
+        out_specs=[pl.BlockSpec(memory_space=pltpu.VMEM)] * 7,
+        scratch_shapes=[
+            pltpu.VMEM(x_dst.shape, BF16),
+            pltpu.VMEM(weight.shape, BF16),
+            pltpu.SemaphoreType.DMA,
+            pltpu.SemaphoreType.DMA,
+        ],
         compiler_params=params,
         cost_estimate=pl.CostEstimate(flops=2 * dest * IN * WIDTH, bytes_accessed=6 << 20, transcendentals=0),
         name="prepare",
@@ -310,7 +331,7 @@
     sources = 2 * x_own.shape[0]
     panels = sources // BLK
     params = pltpu.CompilerParams(vmem_limit_bytes=VMEM_BYTES)
-    ext = 80
+    ext = 72
     operands = (
         x_own, x_other, x_dst, weight, att_src, att_dst,
         proj, grad_t, mask_t, score, self_w, slope, pair,
@@ -327,11 +348,14 @@
         edges,
         out_shape=outs,
         in_specs=[pl.BlockSpec(memory_space=pltpu.SMEM)] * 3
-        + [pl.BlockSpec(memory_space=pltpu.VMEM)] * len(operands),
+        + [
+            pl.BlockSpec(memory_space=pltpu.HBM if o is x_dst or o is weight else pltpu.VMEM)
+            for o in operands
+        ],
         out_specs=[pl.BlockSpec(memory_space=pltpu.VMEM)] * len(outs),
         scratch_shapes=[
             pltpu.VMEM((slots, WIDTH, BLK), BF16),
-            pltpu.VMEM((slots, HEADS, BLK, 2 * BLK), BF16),
+            pltpu.VMEM((slots, HEADS, 2 * BLK, BLK), BF16),
             pltpu.VMEM((dest_blocks, HEADS, ext, 2 * BLK), F32),
             pltpu.VMEM((dest_blocks, HEADS, ext, BLK), BF16),
             pltpu.VMEM((dest_blocks, HEADS, 8, BLK), F32),
@@ -342,6 +366,10 @@
             pltpu.VMEM((slots, BLK, HEADS), F32),
             pltpu.VMEM((WIDTH, LANES), F32),
             pltpu.VMEM((sources, IN), BF16),
+            pltpu.VMEM(x_dst.shape, BF16),
+            pltpu.VMEM(weight.shape, BF16),
+            pltpu.SemaphoreType.DMA,
+            pltpu.SemaphoreType.DMA,
         ],
         compiler_params=params,
         cost_estimate=pl.CostEstimate(flops=4 << 30, bytes_accessed=12 << 20, transcendentals=8 << 20),

time: 109 us -> 108 us (level)
  no operation moved by 1% of the time
where the time goes in v4:
time: 108 us
  blocking collectives  61.8 us (57%)
  Pallas kernels  18.1 us (17%)
  waiting for transfers between devices  11.8 us (11%)
  starting transfers between devices  9.24 us (9%)
  local copies, waits for them, and re-layouts  4.86 us (5%)
    all_to_all x2, blocking collectives, spread(): lax.all_to_all(jnp.broadcast_to(values[None], (count, *values.shape)), ax...  39.7 us
    all_to_all x1, blocking collectives, shards(): got = lax.all_to_all(half, 'panel', 0, 0, axis_index_groups=same_core)  22 us
    pallas_call x1, Pallas kernels, local(): pl.pallas_call(edges, out_shape=outs, in_specs=[pl.BlockSpec(memory_space...  16.5 us
    all_to_all x1, waiting for transfers between devices, spread(): lax.all_to_all(jnp.broadcast_to(values[None], (count, *values.shape)), ax...  9.73 us
    all_to_all x1, starting transfers between devices, spread(): lax.all_to_all(jnp.broadcast_to(values[None], (count, *values.shape)), ax...  6.66 us
    ppermute x1, starting transfers between devices, shards(): x_other = lax.ppermute(x_own, 'panel', siblings)  2.49 us
  transfers between devices with their start and end apart: 3, of which 2 were waited for; matrix products, arithmetic and copies ran while one was open for 1% of the time, Pallas kernels for 2%

profile of v4, /device:TPU:1, one launch (start us, length us, event | category | flops | bytes accessed | tf_op | source)
XLA Modules:
  0.0 107.6 jit_solution(5029329975795095273)
XLA Ops:
  0.6 0.0 copy-start.5
  0.7 1.0 broadcast_in_dim.6
  1.6 0.0 copy-start.6
  1.7 0.0 copy-start.7
  1.7 25.6 %all_to_all.20 = bf16[16,128,128]{2,1,0:T(8,128)(2,1)S(1)} all-to-all(bf16[16,128,128]{2,1,0:T(8,128)(2,1)S(1)} %broadcast_in_dim.6), channel_id=1, replica_groups={{0,16,32,48,64,80,96,112,128,144,160,176,192,208,224,240},{8,24,40,56,7..., dimensions={0} | all-to-all | bytes 1048576 | tf_op jit(solution)/shard_map/all_to_all | solution.py:390
  27.2 2.5 %collective-permute-start = (bf16[2048,128]{1,0:T(8,128)(2,1)S(1)}, bf16[2048,128]{1,0:T(8,128)(2,1)S(1)}, u32[]{:S(2)}, u32[]{:S(2)}) collective-permute-start(bf16[2048,128]{1,0:T(8,128)(2,1)S(1)} %bitcast.19), channel_id=1, source_target_pairs={{0,8},{8,0},{16,24},{24,16},{32,40},{40,32},{48,56},{56,48},{64,72... | collective-permute-start | bytes 1572872 | tf_op jit(solution)/shard_map/ppermute | solution.py:396
  29.7 0.0 copy-start.2
  29.7 0.9 copy-done.2
  30.6 0.9 copy-done.3
  31.5 1.6 %prepare.1 = (bf16[512,512]{1,0:T(8,128)(2,1)S(1)}, bf16[512,512]{1,0:T(8,128)(2,1)S(1)}, f32[16,128,128]{2,1,0:T(8,128)S(1)}, f32[4,8,128]{2,1,0:T(8,128)S(1)},...) custom-call(bf16[512,128]{1,0:T(8,128)(2,1)S(1)} %copy-done.2, bf16[128,512]{1,0:T(8,128)(2,1)S(1)} %copy-done.3, ...), custom_call_target="tpu_custom_call" | custom-call | flops 67108864 | bytes 6291456 | tf_op jit(solution)/shard_map/prepare/pallas_call | solution.py:303
  33.2 0.0 collective-permute-done.x_other_ref
  33.2 16.5 %edges.1 = (f32[512,128]{1,0:T(8,128)}, f32[16,152,128]{2,1,0:T(8,128)S(1)}, bf16[16,152,128]{2,1,0:T(8,128)(2,1)S(1)}) custom-call(s32[16]{0:T(128)S(1)} %copy-done.6, s32[16]{0:T(128)S(1)} %copy-done.7, s32[1]{0:T(128)} %bitcast.place_ref, bf16[2048,128]{1,0:T(8,128)(2,1)S(1)} %bitcast.20, bf16[2048,128]{1,0:T(8,128)(2,1)S(1)} %collective-permute-done.x_other_ref, ...), custom_call_target="tpu_custom_call" | custom-call | flops 4294967296 | bytes 12582912 | tf_op jit(solution)/shard_map/edges/pallas_call | solution.py:347
  49.7 0.1 collective-permute-start.1
  49.8 2.0 %collective-permute-done.1 = bf16[16,152,128]{2,1,0:T(8,128)(2,1)S(1)} collective-permute-done((bf16[16,152,128]{2,1,0:T(8,128)(2,1)S(1)}, bf16[16,152,128]{2,1,0:T(8,128)(2,1)S(1)}, u32[]{:S(2)}, u32[]{:S(2)}) %collective-permute-start.1) | collective-permute-done | bytes 622624 | tf_op jit(solution)/shard_map/ppermute | solution.py:401
  51.9 0.1 add_convert_fusion
  52.0 22.0 %all_to_all.21 = bf16[16,152,128]{2,1,0:T(8,128)(2,1)S(1)} all-to-all(bf16[16,152,128]{2,1,0:T(8,128)(2,1)S(1)} %add_convert_fusion), channel_id=1, replica_groups={{0,16,32,48,64,80,96,112,128,144,160,176,192,208,224,240},{8,24,40,56,7..., dimensions={0} | all-to-all | bytes 1245184 | tf_op jit(solution)/shard_map/all_to_all | solution.py:402
  74.0 0.1 reduce_sum.21
  74.2 14.2 %all_to_all.22 = bf16[8,152,128]{2,1,0:T(8,128)(2,1)S(1)} all-to-all(bf16[8,152,128]{2,1,0:T(8,128)(2,1)S(1)} %broadcast_in_dim.7), channel_id=1, replica_groups=mesh['panel'=32,'rep'=8] {'rep'}, dimensions={0} | all-to-all | bytes 622592 | tf_op jit(solution)/shard_map/all_to_all | solution.py:390
  88.4 0.7 broadcast_in_dim.8
  89.1 6.7 %all-to-all-start.3 = ((bf16[32,24,128]{2,1,0:T(8,128)(2,1)}), bf16[32,24,128]{2,1,0:T(8,128)(2,1)S(1)}, u32[]{:S(2)}, u32[]{:S(2)}) async-start(bf16[32,24,128]{2,1,0:T(8,128)(2,1)} %broadcast_in_dim.8), calls=%async_computation.3 | async-start | bytes 393216 | tf_op jit(solution)/shard_map/all_to_all | solution.py:390
  95.8 0.6 slice.25
  96.4 9.7 %all-to-all-done.3 = bf16[32,24,128]{2,1,0:T(8,128)(2,1)S(1)} async-done(((bf16[32,24,128]{2,1,0:T(8,128)(2,1)}), bf16[32,24,128]{2,1,0:T(8,128)(2,1)S(1)}, u32[]{:S(2)}, u32[]{:S(2)}) %all-to-all-start.3) | async-done | bytes 196640 | tf_op jit(solution)/shard_map/all_to_all | solution.py:390
  106.1 0.7 fusion.1
  106.8 0.7 copy_bitcast_fusion
  (15 shorter events, 0.1 us)
Async XLA Ops:
  0.6 29.1 %copy-start.5 = (f32[8,64]{1,0:T(8,128)S(1)}, f32[8,64]{1,0:T(8,128)}, u32[]{:S(2)}) copy-start(f32[8,64]{1,0:T(8,128)} %att_dst_ref.3) | copy-start | bytes 6148
  0.6 29.1 %copy-start.4 = (f32[8,64]{1,0:T(8,128)S(1)}, f32[8,64]{1,0:T(8,128)}, u32[]{:S(2)}) copy-start(f32[8,64]{1,0:T(8,128)} %att_src_ref.3) | copy-start | bytes 6148
  0.7 29.1 %copy-start = (s32[16,128,128]{2,1,0:T(8,128)S(1)}, s32[16,128,128]{2,1,0:T(8,128)}, u32[]{:S(2)}) copy-start(s32[16,128,128]{2,1,0:T(8,128)} %mask_ref.1) | copy-start | bytes 3145732
  0.7 29.1 %copy-start.1 = (bf16[512,512]{1,0:T(8,128)(2,1)S(1)}, bf16[512,512]{1,0:T(8,128)(2,1)}, u32[]{:S(2)}) copy-start(bf16[512,512]{1,0:T(8,128)(2,1)} %grad_ref.1) | copy-start | bytes 1572868
  1.6 31.6 %copy-start.6 = (s32[16]{0:T(128)S(1)}, s32[16]{0:T(128)}, u32[]{:S(2)}) copy-start(s32[16]{0:T(128)} %rows_ref.1) | copy-start | bytes 196
  1.7 31.6 %copy-start.7 = (s32[16]{0:T(128)S(1)}, s32[16]{0:T(128)}, u32[]{:S(2)}) copy-start(s32[16]{0:T(128)} %cols_ref.1) | copy-start | bytes 196
  27.2 6.0 %collective-permute-start = (bf16[2048,128]{1,0:T(8,128)(2,1)S(1)}, bf16[2048,128]{1,0:T(8,128)(2,1)S(1)}, u32[]{:S(2)}, u32[]{:S(2)}) collective-permute-start(bf16[2048,128]{1,0:T(8,128)(2,1)S(1)} %bitcast.19), channel_id=1, source_target_pairs={{0,8},{8,0},{16,24},{24,16},{32,40},{40,32},{48,56},{56,48},{64,72... | collective-permute-start | bytes 1572872 | tf_op jit(solution)/shard_map/ppermute | solution.py:396
  29.7 0.9 copy-start.2
  30.6 0.9 copy-start.3
  49.7 2.1 %collective-permute-start.1 = (bf16[16,152,128]{2,1,0:T(8,128)(2,1)S(1)}, bf16[16,152,128]{2,1,0:T(8,128)(2,1)S(1)}, u32[]{:S(2)}, u32[]{:S(2)}) collective-permute-start(bf16[16,152,128]{2,1,0:T(8,128)(2,1)S(1)} %get-tuple-element.23), channel_id=1, source_target_pairs={{0,8},{8,0},{16,24},{24,16},{32,40},{40,32},{48,56},{56,48},{64,72... | collective-permute-start | bytes 1867784 | tf_op jit(solution)/shard_map/ppermute | solution.py:401
  89.1 17.0 %all-to-all-start.3 = ((bf16[32,24,128]{2,1,0:T(8,128)(2,1)}), bf16[32,24,128]{2,1,0:T(8,128)(2,1)S(1)}, u32[]{:S(2)}, u32[]{:S(2)}) async-start(bf16[32,24,128]{2,1,0:T(8,128)(2,1)} %broadcast_in_dim.8), calls=%async_computation.3 | async-start | bytes 393216 | tf_op jit(solution)/shard_map/all_to_all | solution.py:390

commit v5 on v4

--- a/solution.py
+++ b/solution.py
@@ -176,16 +176,19 @@
             feats = slice(h * HEAD_DIM, (h + 1) * HEAD_DIM)
             sums = acc[r, h]
             w_self = self_w[h : h + 1]
-            inv = 1.0 / (sums[HEAD_DIM : HEAD_DIM + 1, :BLK] + w_self)
+            denom = sums[HEAD_DIM : HEAD_DIM + 1, :BLK] + w_self
+            inv = 1.0 / denom
+            power = jnp.exp2(-jnp.round(jnp.log2(denom))).astype(BF16).astype(F32)
+            near = 1.0 / (denom * power)
             numer = sums[:HEAD_DIM, :BLK] + w_self * proj_ref[feats, lanes].astype(F32)
             grad = grad_t_ref[feats, lanes].astype(F32)
-            part = (grad * inv).astype(BF16)
+            part = (grad * near).astype(BF16)
             part_wide = part.astype(F32)
             centred = jnp.sum(grad * numer, axis=0, keepdims=True) * inv
             centred_part = jnp.sum(part_wide * numer, axis=0, keepdims=True) * inv
             grad_d = (
-                jnp.sum(part_wide * sums[:HEAD_DIM, BLK:], axis=0, keepdims=True)
-                - centred_part * sums[HEAD_DIM : HEAD_DIM + 1, BLK:]
+                jnp.sum(part_wide * (sums[:HEAD_DIM, BLK:] * power), axis=0, keepdims=True)
+                - centred_part * (sums[HEAD_DIM : HEAD_DIM + 1, BLK:] * power)
             )
             att_self = w_self * inv
             grad_self = (
@@ -195,6 +198,7 @@
             c_hi, c_lo = split2(centred_part)
             scaled_c[r, h, 0:1] = c_hi.astype(F32)
             scaled_c[r, h, 1:2] = c_lo.astype(F32)
+            scaled_c[r, h, 2:3] = power
             selfs.append(att_self)
             grads.append(grad_self)
             dsts.append(grad_d + grad_self)
@@ -230,7 +234,8 @@
         proj = proj_src[b]
         feats, grads = [], []
         for h in range(HEADS):
-            out = mm(scaled[row, h], tiles[b, h], NT)
+            power = scaled_c[row, h, 2:3].astype(BF16)
+            out = mm(scaled[row, h], tiles[b, h] * power, NT)
             feats.append(out[:HEAD_DIM, :BLK])
             proj_h = proj[h * HEAD_DIM : (h + 1) * HEAD_DIM].astype(F32)
             grads.append(

time: 108 us -> 108 us (level)
  no operation moved by 1% of the time
where the time goes in v5:
time: 108 us
  blocking collectives  61.8 us (57%)
  Pallas kernels  18.3 us (17%)
  waiting for transfers between devices  11.8 us (11%)
  starting transfers between devices  9.24 us (9%)
  local copies, waits for them, and re-layouts  4.86 us (5%)
    all_to_all x2, blocking collectives, spread(): lax.all_to_all(jnp.broadcast_to(values[None], (count, *values.shape)), ax...  39.7 us
    all_to_all x1, blocking collectives, shards(): got = lax.all_to_all(half, 'panel', 0, 0, axis_index_groups=same_core)  22.1 us
    pallas_call x1, Pallas kernels, local(): pl.pallas_call(edges, out_shape=outs, in_specs=[pl.BlockSpec(memory_space...  16.7 us
    all_to_all x1, waiting for transfers between devices, spread(): lax.all_to_all(jnp.broadcast_to(values[None], (count, *values.shape)), ax...  9.73 us
    all_to_all x1, starting transfers between devices, spread(): lax.all_to_all(jnp.broadcast_to(values[None], (count, *values.shape)), ax...  6.66 us
    ppermute x1, starting transfers between devices, shards(): x_other = lax.ppermute(x_own, 'panel', siblings)  2.49 us
  transfers between devices with their start and end apart: 3, of which 2 were waited for; matrix products, arithmetic and copies ran while one was open for 1% of the time, Pallas kernels for 2%

profile of v5, /device:TPU:1, one launch (start us, length us, event | category | flops | bytes accessed | tf_op | source)
XLA Modules:
  0.0 107.7 jit_solution(10027934277967881709)
XLA Ops:
  0.6 0.0 copy-start.5
  0.7 1.0 broadcast_in_dim.6
  1.6 0.0 copy-start.6
  1.7 0.0 copy-start.7
  1.7 25.6 %all_to_all.20 = bf16[16,128,128]{2,1,0:T(8,128)(2,1)S(1)} all-to-all(bf16[16,128,128]{2,1,0:T(8,128)(2,1)S(1)} %broadcast_in_dim.6), channel_id=1, replica_groups={{0,16,32,48,64,80,96,112,128,144,160,176,192,208,224,240},{8,24,40,56,7..., dimensions={0} | all-to-all | bytes 1048576 | tf_op jit(solution)/shard_map/all_to_all | solution.py:395
  27.2 2.5 %collective-permute-start = (bf16[2048,128]{1,0:T(8,128)(2,1)S(1)}, bf16[2048,128]{1,0:T(8,128)(2,1)S(1)}, u32[]{:S(2)}, u32[]{:S(2)}) collective-permute-start(bf16[2048,128]{1,0:T(8,128)(2,1)S(1)} %bitcast.19), channel_id=1, source_target_pairs={{0,8},{8,0},{16,24},{24,16},{32,40},{40,32},{48,56},{56,48},{64,72... | collective-permute-start | bytes 1572872 | tf_op jit(solution)/shard_map/ppermute | solution.py:401
  29.7 0.0 copy-start.2
  29.7 0.9 copy-done.2
  30.6 0.9 copy-done.3
  31.5 1.6 %prepare.1 = (bf16[512,512]{1,0:T(8,128)(2,1)S(1)}, bf16[512,512]{1,0:T(8,128)(2,1)S(1)}, f32[16,128,128]{2,1,0:T(8,128)S(1)}, f32[4,8,128]{2,1,0:T(8,128)S(1)},...) custom-call(bf16[512,128]{1,0:T(8,128)(2,1)S(1)} %copy-done.2, bf16[128,512]{1,0:T(8,128)(2,1)S(1)} %copy-done.3, ...), custom_call_target="tpu_custom_call" | custom-call | flops 67108864 | bytes 6291456 | tf_op jit(solution)/shard_map/prepare/pallas_call | solution.py:308
  33.2 0.0 collective-permute-done.x_other_ref
  33.2 16.7 %edges.1 = (f32[512,128]{1,0:T(8,128)}, f32[16,152,128]{2,1,0:T(8,128)S(1)}, bf16[16,152,128]{2,1,0:T(8,128)(2,1)S(1)}) custom-call(s32[16]{0:T(128)S(1)} %copy-done.6, s32[16]{0:T(128)S(1)} %copy-done.7, s32[1]{0:T(128)} %bitcast.place_ref, bf16[2048,128]{1,0:T(8,128)(2,1)S(1)} %bitcast.20, bf16[2048,128]{1,0:T(8,128)(2,1)S(1)} %collective-permute-done.x_other_ref, ...), custom_call_target="tpu_custom_call" | custom-call | flops 4294967296 | bytes 12582912 | tf_op jit(solution)/shard_map/edges/pallas_call | solution.py:352
  49.9 0.1 collective-permute-start.1
  50.0 2.0 %collective-permute-done.1 = bf16[16,152,128]{2,1,0:T(8,128)(2,1)S(1)} collective-permute-done((bf16[16,152,128]{2,1,0:T(8,128)(2,1)S(1)}, bf16[16,152,128]{2,1,0:T(8,128)(2,1)S(1)}, u32[]{:S(2)}, u32[]{:S(2)}) %collective-permute-start.1) | collective-permute-done | bytes 622624 | tf_op jit(solution)/shard_map/ppermute | solution.py:406
  52.0 0.1 add_convert_fusion
  52.2 22.1 %all_to_all.21 = bf16[16,152,128]{2,1,0:T(8,128)(2,1)S(1)} all-to-all(bf16[16,152,128]{2,1,0:T(8,128)(2,1)S(1)} %add_convert_fusion), channel_id=1, replica_groups={{0,16,32,48,64,80,96,112,128,144,160,176,192,208,224,240},{8,24,40,56,7..., dimensions={0} | all-to-all | bytes 1245184 | tf_op jit(solution)/shard_map/all_to_all | solution.py:407
  74.3 0.1 reduce_sum.21
  74.4 14.1 %all_to_all.22 = bf16[8,152,128]{2,1,0:T(8,128)(2,1)S(1)} all-to-all(bf16[8,152,128]{2,1,0:T(8,128)(2,1)S(1)} %broadcast_in_dim.7), channel_id=1, replica_groups=mesh['panel'=32,'rep'=8] {'rep'}, dimensions={0} | all-to-all | bytes 622592 | tf_op jit(solution)/shard_map/all_to_all | solution.py:395
  88.6 0.7 broadcast_in_dim.8
  89.3 6.7 %all-to-all-start.3 = ((bf16[32,24,128]{2,1,0:T(8,128)(2,1)}), bf16[32,24,128]{2,1,0:T(8,128)(2,1)S(1)}, u32[]{:S(2)}, u32[]{:S(2)}) async-start(bf16[32,24,128]{2,1,0:T(8,128)(2,1)} %broadcast_in_dim.8), calls=%async_computation.3 | async-start | bytes 393216 | tf_op jit(solution)/shard_map/all_to_all | solution.py:395
  96.0 0.6 slice.25
  96.6 9.7 %all-to-all-done.3 = bf16[32,24,128]{2,1,0:T(8,128)(2,1)S(1)} async-done(((bf16[32,24,128]{2,1,0:T(8,128)(2,1)}), bf16[32,24,128]{2,1,0:T(8,128)(2,1)S(1)}, u32[]{:S(2)}, u32[]{:S(2)}) %all-to-all-start.3) | async-done | bytes 196640 | tf_op jit(solution)/shard_map/all_to_all | solution.py:395
  106.3 0.7 fusion.1
  107.0 0.7 copy_bitcast_fusion
  (15 shorter events, 0.1 us)
Async XLA Ops:
  0.6 29.1 %copy-start.5 = (f32[8,64]{1,0:T(8,128)S(1)}, f32[8,64]{1,0:T(8,128)}, u32[]{:S(2)}) copy-start(f32[8,64]{1,0:T(8,128)} %att_dst_ref.3) | copy-start | bytes 6148
  0.6 29.1 %copy-start.4 = (f32[8,64]{1,0:T(8,128)S(1)}, f32[8,64]{1,0:T(8,128)}, u32[]{:S(2)}) copy-start(f32[8,64]{1,0:T(8,128)} %att_src_ref.3) | copy-start | bytes 6148
  0.7 29.1 %copy-start = (s32[16,128,128]{2,1,0:T(8,128)S(1)}, s32[16,128,128]{2,1,0:T(8,128)}, u32[]{:S(2)}) copy-start(s32[16,128,128]{2,1,0:T(8,128)} %mask_ref.1) | copy-start | bytes 3145732
  0.7 29.1 %copy-start.1 = (bf16[512,512]{1,0:T(8,128)(2,1)S(1)}, bf16[512,512]{1,0:T(8,128)(2,1)}, u32[]{:S(2)}) copy-start(bf16[512,512]{1,0:T(8,128)(2,1)} %grad_ref.1) | copy-start | bytes 1572868
  1.6 31.6 %copy-start.6 = (s32[16]{0:T(128)S(1)}, s32[16]{0:T(128)}, u32[]{:S(2)}) copy-start(s32[16]{0:T(128)} %rows_ref.1) | copy-start | bytes 196
  1.7 31.6 %copy-start.7 = (s32[16]{0:T(128)S(1)}, s32[16]{0:T(128)}, u32[]{:S(2)}) copy-start(s32[16]{0:T(128)} %cols_ref.1) | copy-start | bytes 196
  27.2 6.0 %collective-permute-start = (bf16[2048,128]{1,0:T(8,128)(2,1)S(1)}, bf16[2048,128]{1,0:T(8,128)(2,1)S(1)}, u32[]{:S(2)}, u32[]{:S(2)}) collective-permute-start(bf16[2048,128]{1,0:T(8,128)(2,1)S(1)} %bitcast.19), channel_id=1, source_target_pairs={{0,8},{8,0},{16,24},{24,16},{32,40},{40,32},{48,56},{56,48},{64,72... | collective-permute-start | bytes 1572872 | tf_op jit(solution)/shard_map/ppermute | solution.py:401
  29.7 0.9 copy-start.2
  30.6 0.9 copy-start.3
  49.9 2.1 %collective-permute-start.1 = (bf16[16,152,128]{2,1,0:T(8,128)(2,1)S(1)}, bf16[16,152,128]{2,1,0:T(8,128)(2,1)S(1)}, u32[]{:S(2)}, u32[]{:S(2)}) collective-permute-start(bf16[16,152,128]{2,1,0:T(8,128)(2,1)S(1)} %get-tuple-element.23), channel_id=1, source_target_pairs={{0,8},{8,0},{16,24},{24,16},{32,40},{40,32},{48,56},{56,48},{64,72... | collective-permute-start | bytes 1867784 | tf_op jit(solution)/shard_map/ppermute | solution.py:406
  89.3 17.0 %all-to-all-start.3 = ((bf16[32,24,128]{2,1,0:T(8,128)(2,1)}), bf16[32,24,128]{2,1,0:T(8,128)(2,1)S(1)}, u32[]{:S(2)}, u32[]{:S(2)}) async-start(bf16[32,24,128]{2,1,0:T(8,128)(2,1)} %broadcast_in_dim.8), calls=%async_computation.3 | async-start | bytes 393216 | tf_op jit(solution)/shard_map/all_to_all | solution.py:395
